TPU v7x, 32 devices: a whole 2x2x4 slice. The times are simulated.
32 devices in a mesh: dp: 16 (over z, x, core), mp: 2 (over y).
Axes of the slice: x: 2, y: 2, z: 4, core: 2. Of those that a mesh axis runs over, the one named last changes fastest.
Arguments:
- tokens: bfloat16 [16384, 1024], P('dp'), may hold values from -60 to 60
- w_query: bfloat16 [1024, 1024], P('dp', 'mp'), may hold values from -0.25 to 0.25
- w_key: bfloat16 [1024, 1024], P('dp', 'mp'), may hold values from -0.25 to 0.25
- w_value: bfloat16 [1024, 1024], P('dp', 'mp'), may hold values from -0.1875 to 0.1875
- w_out: bfloat16 [1024, 1024], P('mp', 'dp'), may hold values from -0.5 to 0.5
- w_gate: bfloat16 [1024, 2816], P('dp', 'mp'), may hold values from -0.1875 to 0.1875
- w_up: bfloat16 [1024, 2816], P('dp', 'mp'), may hold values from -0.1875 to 0.1875
- w_down: bfloat16 [2816, 1024], P('mp', 'dp'), may hold values from -0.109375 to 0.109375
- out_grad: bfloat16 [16384, 1024], P('dp'), may hold values from -6 to 6
Outputs:
- block_out: bfloat16 [16384, 1024], P('dp')
- grad_tokens: bfloat16 [16384, 1024], P('dp')
- grad_query: float32 [1024, 1024], P('dp', 'mp')
- grad_key: float32 [1024, 1024], P('dp', 'mp')
- grad_value: float32 [1024, 1024], P('dp', 'mp')
- grad_out: float32 [1024, 1024], P('mp', 'dp')
- grad_gate: float32 [1024, 2816], P('dp', 'mp')
- grad_up: float32 [1024, 2816], P('dp', 'mp')
- grad_down: float32 [2816, 1024], P('mp', 'dp')
All inputs are finite; a program needn't handle non-finite values.
Results may differ from a plain program's by a relative error of at most 0.014.
Values may be sent and summed in bfloat16 or wider, within the bound.
A program may use at most 128 MiB of HBM per device.

v0:
```python
import jax
import jax.numpy as jnp
from jax import lax
from jax.sharding import PartitionSpec as P

HEADS = 16
BLK = 64
MICRO = 2


eps = 1e-06


def normalize(values_in):
    factor = lax.rsqrt(jnp.mean(values_in * values_in, axis=-1, keepdims=True) + eps)
    return (values_in * factor, factor)


def norm_back(grad_normed, normed, factor):
    return factor * (grad_normed - normed * jnp.mean(grad_normed * normed, axis=-1, keepdims=True))


def contract_rows(left, right):
    return lax.dot_general(
        left, right, (((0,), (0,)), ((), ())), preferred_element_type=jnp.float32
    )


def times_transposed(left, right):
    return lax.dot_general(
        left, right, (((1,), (1,)), ((), ())), preferred_element_type=jnp.float32
    )


def forward_product(left, right):
    return jnp.dot(left, right, preferred_element_type=jnp.float32)


def layer_pass(tokens_part, grad_part, weights):
    w_query, w_key, w_value, w_out, w_gate, w_up, w_down = weights
    count = tokens_part.shape[0]
    width = tokens_part.shape[1]
    head_dim = width // HEADS
    local = w_query.shape[1] // head_dim
    blocks = count // BLK
    scale = head_dim ** (-0.5)
    places = jnp.arange(BLK)
    causal = places[:, None] >= places[None, :]

    def split_heads(matrix):
        return matrix.reshape(blocks, BLK, local, head_dim).transpose(0, 2, 1, 3)

    def join_heads(stacked):
        return stacked.transpose(0, 2, 1, 3).reshape(count, local * head_dim)

    def scores_of(query, keys):
        raw = jnp.einsum("bhqd,bhkd->bhqk", query, keys, preferred_element_type=jnp.float32) * scale
        return jnp.where(causal, raw, -1e30)

    tokens_float = tokens_part.astype(jnp.float32)
    norm_one, factor_one = normalize(tokens_float)
    input_one = norm_one.astype(jnp.bfloat16)
    query = split_heads(forward_product(input_one, w_query).astype(jnp.bfloat16))
    keys = split_heads(forward_product(input_one, w_key).astype(jnp.bfloat16))
    values = split_heads(forward_product(input_one, w_value).astype(jnp.bfloat16))
    scores = scores_of(query, keys)
    peak = jnp.max(scores, axis=-1, keepdims=True)
    raised = jnp.exp(scores - peak)
    totals = jnp.sum(raised, axis=-1, keepdims=True)
    log_total = peak + jnp.log(totals)
    attend_low = (raised / totals).astype(jnp.bfloat16)
    mixed_heads = jnp.einsum(
        "bhqk,bhkd->bhqd", attend_low, values, preferred_element_type=jnp.float32
    )
    mixed = join_heads(mixed_heads.astype(jnp.bfloat16))
    branch_one = lax.psum(forward_product(mixed, w_out), "mp")
    resid = tokens_float + branch_one
    norm_two, factor_two = normalize(resid)
    input_two = norm_two.astype(jnp.bfloat16)
    gate = forward_product(input_two, w_gate)
    upper = forward_product(input_two, w_up)
    hidden = (gate * upper).astype(jnp.bfloat16)
    grad_down = contract_rows(hidden, grad_part)
    grad_hidden = times_transposed(grad_part, w_down)
    gate_back = (grad_hidden * upper).astype(jnp.bfloat16)
    up_back = (grad_hidden * gate).astype(jnp.bfloat16)
    grad_gate = contract_rows(input_two, gate_back)
    grad_up = contract_rows(input_two, up_back)
    two_partial = times_transposed(gate_back, w_gate) + times_transposed(up_back, w_up)
    branch_two = lax.psum(forward_product(hidden, w_down).astype(jnp.bfloat16), "mp").astype(
        jnp.float32
    )
    block_out = (resid + branch_two).astype(jnp.bfloat16)
    norm_two_back = lax.psum(two_partial, "mp")
    resid_back = grad_part.astype(jnp.float32) + norm_back(norm_two_back, norm_two, factor_two)
    branch_back = resid_back.astype(jnp.bfloat16)
    grad_out = contract_rows(mixed, branch_back)
    mixed_back = split_heads(times_transposed(branch_back, w_out).astype(jnp.bfloat16))
    attend = jnp.exp(scores_of(query, keys) - log_total)
    values_back = jnp.einsum(
        "bhqk,bhqd->bhkd", attend_low, mixed_back, preferred_element_type=jnp.float32
    )
    values_back = join_heads(values_back.astype(jnp.bfloat16))
    attend_back = jnp.einsum(
        "bhqd,bhkd->bhqk", mixed_back, values, preferred_element_type=jnp.float32
    )
    scores_back = attend * (attend_back - jnp.sum(attend_back * attend, axis=-1, keepdims=True))
    scores_back = scores_back.astype(jnp.bfloat16)
    query_back = scale * jnp.einsum(
        "bhqk,bhkd->bhqd", scores_back, keys, preferred_element_type=jnp.float32
    )
    query_back = join_heads(query_back.astype(jnp.bfloat16))
    keys_back = scale * jnp.einsum(
        "bhqk,bhqd->bhkd", scores_back, query, preferred_element_type=jnp.float32
    )
    keys_back = join_heads(keys_back.astype(jnp.bfloat16))
    grad_query = contract_rows(input_one, query_back)
    grad_key = contract_rows(input_one, keys_back)
    grad_value = contract_rows(input_one, values_back)
    one_partial = (
        times_transposed(query_back, w_query)
        + times_transposed(keys_back, w_key)
        + times_transposed(values_back, w_value)
    )
    norm_one_back = lax.psum(one_partial, "mp")
    grad_tokens = (resid_back + norm_back(norm_one_back, norm_one, factor_one)).astype(jnp.bfloat16)
    return (
        block_out,
        grad_tokens,
        (grad_query, grad_key, grad_value, grad_out, grad_gate, grad_up, grad_down),
    )


def body(tokens, w_query, w_key, w_value, w_out, w_gate, w_up, w_down, out_grad):
    count = tokens.shape[0] // MICRO
    outputs = []
    backs = []
    summed = None
    for number in range(MICRO):
        weights = (
            lax.all_gather(w_query, "dp", axis=0, tiled=True),
            lax.all_gather(w_key, "dp", axis=0, tiled=True),
            lax.all_gather(w_value, "dp", axis=0, tiled=True),
            lax.all_gather(w_out, "dp", axis=1, tiled=True),
            lax.all_gather(w_gate, "dp", axis=0, tiled=True),
            lax.all_gather(w_up, "dp", axis=0, tiled=True),
            lax.all_gather(w_down, "dp", axis=1, tiled=True),
        )
        first = number * count
        block_out, grad_tokens, grads = layer_pass(
            tokens[first : first + count], out_grad[first : first + count], weights
        )
        outputs.append(block_out)
        backs.append(grad_tokens)
        if number == 0:
            summed = tuple(grads)
        else:
            summed = tuple(jax.tree.map(jnp.add, tuple(summed), tuple(grads)))
    summed = (
        lax.psum_scatter(summed[0], "dp", scatter_dimension=0, tiled=True),
        lax.psum_scatter(summed[1], "dp", scatter_dimension=0, tiled=True),
        lax.psum_scatter(summed[2], "dp", scatter_dimension=0, tiled=True),
        lax.psum_scatter(summed[3], "dp", scatter_dimension=1, tiled=True),
        lax.psum_scatter(summed[4], "dp", scatter_dimension=0, tiled=True),
        lax.psum_scatter(summed[5], "dp", scatter_dimension=0, tiled=True),
        lax.psum_scatter(summed[6], "dp", scatter_dimension=1, tiled=True),
    )
    return (
        jnp.concatenate(outputs, axis=0),
        jnp.concatenate(backs, axis=0),
        summed[0],
        summed[1],
        summed[2],
        summed[3],
        summed[4],
        summed[5],
        summed[6],
    )


def solution(mesh):
    in_specs = (
        P("dp", None),
        P("dp", "mp"),
        P("dp", "mp"),
        P("dp", "mp"),
        P("mp", "dp"),
        P("dp", "mp"),
        P("dp", "mp"),
        P("mp", "dp"),
        P("dp", None),
    )
    out_specs = (
        P("dp", None),
        P("dp", None),
        P("dp", "mp"),
        P("dp", "mp"),
        P("dp", "mp"),
        P("mp", "dp"),
        P("dp", "mp"),
        P("dp", "mp"),
        P("mp", "dp"),
    )
    return jax.shard_map(body, mesh=mesh, in_specs=in_specs, out_specs=out_specs, check_vma=False)
```

profile of v0, /device:TPU:0, one launch (start us, length us, event | category | flops | bytes accessed | tf_op | source)
XLA Modules:
  0.0 1340.7 jit_solution(5174192566479510309)
XLA Ops:
  11.6 39.2 %all-gather.8.cloned.1.call-done = bf16[1024,512]{1,0:T(8,128)(2,1)} async-done(((bf16[64,512]{1,0:T(8,128)(2,1)}), bf16[1024,512]{1,0:T(8,128)(2,1)}) %all-gather.8.cloned.1.call-update) | async-done | bytes 1048592 | tf_op jit(solution)/shard_map/all_gather | solution.py:141
  50.7 3.1 convolution_convert_fusion.13
  55.5 34.3 %all-gather.10.cloned.1.call-done = bf16[1024,512]{1,0:T(8,128)(2,1)} async-done(((bf16[64,512]{1,0:T(8,128)(2,1)}), bf16[1024,512]{1,0:T(8,128)(2,1)}) %all-gather.10.cloned.1.call-update) | async-done | bytes 1048592 | tf_op jit(solution)/shard_map/all_gather | solution.py:142
  89.7 2.8 convolution_convert_fusion.12
  94.9 33.9 %all-gather.12.cloned.1.call-done = bf16[1024,512]{1,0:T(8,128)(2,1)} async-done(((bf16[64,512]{1,0:T(8,128)(2,1)}), bf16[1024,512]{1,0:T(8,128)(2,1)}) %all-gather.12.cloned.1.call-update) | async-done | bytes 1048592 | tf_op jit(solution)/shard_map/all_gather | solution.py:143
  128.8 2.8 convolution_convert_fusion.11
  142.1 25.5 %all-gather.14.cloned.1.call-done = bf16[512,1024]{0,1:T(8,128)(2,1)} async-done(((bf16[512,64]{0,1:T(8,128)(2,1)}), bf16[512,1024]{0,1:T(8,128)(2,1)}) %all-gather.14.cloned.1.call-update) | async-done | bytes 1048592 | tf_op jit(solution)/shard_map/all_gather | solution.py:144
  167.6 3.3 fusion.91
  173.6 59.4 %all-reduce.9.cloned.1.call-done = f32[512,1024]{1,0:T(8,128)} async-done(((f32[512,1024]{1,0:T(8,128)}), f32[512,1024]{1,0:T(8,128)}) %all-reduce.9.cloned.1.call-update) | async-done | bytes 2097168 | tf_op jit(solution)/shard_map/psum | solution.py:76
  239.1 2.9 convolution_convert_fusion.9
  247.6 2.6 fusion.90
  253.2 2.7 reshape.143
  256.0 3.2 fusion.93
  260.5 18.7 %all-gather.18.cloned.1.call-done = bf16[1024,1408]{1,0:T(8,128)(2,1)} async-done(((bf16[64,1408]{1,0:T(8,128)(2,1)}), bf16[1024,1408]{1,0:T(8,128)(2,1)}) %all-gather.18.cloned.1.call-update) | async-done | bytes 2883600 | tf_op jit(solution)/shard_map/all_gather | solution.py:146
  279.2 5.5 fusion.92
  284.6 39.4 %all-gather.20.cloned.1.call-done = bf16[1408,1024]{0,1:T(8,128)(2,1)} async-done(((bf16[1408,64]{0,1:T(8,128)(2,1)}), bf16[1408,1024]{0,1:T(8,128)(2,1)}) %all-gather.20.cloned.1.call-update) | async-done | bytes 2883600 | tf_op jit(solution)/shard_map/all_gather | solution.py:147
  324.1 5.5 fusion.67
  329.6 39.4 %all-gather.16.cloned.1.call-done = bf16[1024,1408]{1,0:T(8,128)(2,1)} async-done(((bf16[64,1408]{1,0:T(8,128)(2,1)}), bf16[1024,1408]{1,0:T(8,128)(2,1)}) %all-gather.16.cloned.1.call-update) | async-done | bytes 2883600 | tf_op jit(solution)/shard_map/all_gather | solution.py:145
  369.0 7.1 multiply_convert_fusion.5
  378.9 3.2 convolution_add_fusion.8
  382.3 5.1 convolution_convert_fusion.4
  387.4 101.4 %all-reduce.15.cloned.1.call-done = (f32[512,1024]{1,0:T(8,128)}, f32[512,1024]{1,0:T(8,128)}) async-done(((f32[512,1024]{1,0:T(8,128)}, f32[512,1024]{1,0:T(8,128)}), (f32[512,1024]{1,0:T(8,128)}, f32[512,1024]{1,0:T(8,128)})) %all-reduce.15.cloned.1.call-update) | async-done | bytes 4194320 | tf_op jit(solution)/shard_map/psum | solution.py:94
  488.8 3.7 multiply_reduce_fusion.3
  499.0 3.5 multiply_convert_fusion
  503.6 2.8 convolution_convert_fusion.2
  506.6 4.2 fusion.99
  510.8 3.1 convolution_add_fusion.7
  513.9 55.6 %all-reduce.17.cloned.1.call-done = (bf16[512,1024]{1,0:T(8,128)(2,1)}, bf16[512,1024]{1,0:T(8,128)(2,1)}) async-done(((bf16[512,1024]{1,0:T(8,128)(2,1)}, bf16[512,1024]{1,0:T(8,128)(2,1)}), (bf16[512,1024]{1,0:T(8,128)(2,1)}, bf16[512,1024]{1,0:T(8,128)(2,1)})) %all-reduce.17.cloned.1.call-update) | async-done | bytes 2097168 | tf_op jit(solution)/shard_map/psum | solution.py:90
  569.6 4.6 multiply_add_fusion.1
  577.0 2.8 reshape.144
  608.1 108.0 %all-reduce.13.cloned.1.call-done = (f32[512,1024]{1,0:T(8,128)}, f32[512,1024]{1,0:T(8,128)}) async-done(((f32[512,1024]{1,0:T(8,128)}, f32[512,1024]{1,0:T(8,128)}), (f32[512,1024]{1,0:T(8,128)}, f32[512,1024]{1,0:T(8,128)})) %all-reduce.13.cloned.1.call-update) | async-done | bytes 4194320 | tf_op jit(solution)/shard_map/psum | solution.py:94
  716.1 3.8 fusion.11
  721.4 3.7 multiply_add_fusion
  754.8 3.6 fusion.103
  758.5 4.4 convolution_add_fusion.1
  763.0 3.6 fusion.102
  766.6 4.4 convolution_add_fusion.2
  771.2 3.6 fusion.65
  774.8 4.3 convolution_add_fusion
  798.3 2.7 pad_maximum_fusion
  801.0 16.6 %all-reduce.11.cloned.1.call-done = f32[512,1024]{1,0:T(8,128)} async-done(((f32[512,1024]{1,0:T(8,128)}), f32[512,1024]{1,0:T(8,128)}) %all-reduce.11.cloned.1.call-update) | async-done | bytes 2097168 | tf_op jit(solution)/shard_map/psum | solution.py:125
  823.6 80.0 %reduce-scatter.18.cloned.1.call-done = f32[64,1408]{1,0:T(8,128)} async-done(((f32[1024,1408]{1,0:T(8,128)}), f32[64,1408]{1,0:T(8,128)}) %reduce-scatter.18.cloned.1.call-update) | async-done | bytes 360464 | tf_op jit(solution)/shard_map/reduce_scatter | solution.py:165
  903.6 85.0 %reduce-scatter.16.cloned.1.call-done = f32[64,1408]{1,0:T(8,128)} async-done(((f32[1024,1408]{1,0:T(8,128)}), f32[64,1408]{1,0:T(8,128)}) %reduce-scatter.16.cloned.1.call-update) | async-done | bytes 360464 | tf_op jit(solution)/shard_map/reduce_scatter | solution.py:164
  988.6 85.0 %reduce-scatter.20.cloned.1.call-done = f32[1408,64]{0,1:T(8,128)} async-done(((f32[1408,1024]{0,1:T(8,128)}), f32[1408,64]{0,1:T(8,128)}) %reduce-scatter.20.cloned.1.call-update) | async-done | bytes 360464 | tf_op jit(solution)/shard_map/reduce_scatter | solution.py:166
  1073.6 65.2 %reduce-scatter.14.cloned.1.call-done = f32[512,64]{0,1:T(8,128)} async-done(((f32[512,1024]{0,1:T(8,128)}), f32[512,64]{0,1:T(8,128)}) %reduce-scatter.14.cloned.1.call-update) | async-done | bytes 131088 | tf_op jit(solution)/shard_map/reduce_scatter | solution.py:163
  1138.8 64.9 %reduce-scatter.12.cloned.1.call-done = f32[64,512]{1,0:T(8,128)} async-done(((f32[1024,512]{1,0:T(8,128)}), f32[64,512]{1,0:T(8,128)}) %reduce-scatter.12.cloned.1.call-update) | async-done | bytes 131088 | tf_op jit(solution)/shard_map/reduce_scatter | solution.py:162
  1203.7 64.9 %reduce-scatter.10.cloned.1.call-done = f32[64,512]{1,0:T(8,128)} async-done(((f32[1024,512]{1,0:T(8,128)}), f32[64,512]{1,0:T(8,128)}) %reduce-scatter.10.cloned.1.call-update) | async-done | bytes 131088 | tf_op jit(solution)/shard_map/reduce_scatter | solution.py:161
  1268.6 65.1 %reduce-scatter.8.cloned.1.call-done = f32[64,512]{1,0:T(8,128)} async-done(((f32[1024,512]{1,0:T(8,128)}), f32[64,512]{1,0:T(8,128)}) %reduce-scatter.8.cloned.1.call-update) | async-done | bytes 131088 | tf_op jit(solution)/shard_map/reduce_scatter | solution.py:160
  (243 shorter events, 135.4 us)
Async XLA Ops:
  7.2 43.6 %all-gather.8.cloned.1.call-start = ((), (), s32[]{:S(2)}) async-start(), calls=%async_computation.7 | async-start | bytes 1114112 | tf_op jit(solution)/shard_map/all_gather | solution.py:141
  7.9 81.8 %all-gather.10.cloned.1.call-start = ((), (), s32[]{:S(2)}) async-start(), calls=%async_computation.8 | async-start | bytes 1114112 | tf_op jit(solution)/shard_map/all_gather | solution.py:142
  8.7 120.1 %all-gather.12.cloned.1.call-start = ((), (), s32[]{:S(2)}) async-start(), calls=%async_computation.9 | async-start | bytes 1114112 | tf_op jit(solution)/shard_map/all_gather | solution.py:143
  9.4 158.2 %all-gather.14.cloned.1.call-start = ((), (), s32[]{:S(2)}) async-start(), calls=%async_computation.10 | async-start | bytes 1114112 | tf_op jit(solution)/shard_map/all_gather | solution.py:144
  10.0 223.1 %all-reduce.9.cloned.1.call-start = ((), (), s32[]{:S(2)}) async-start(), calls=%async_computation.11 | async-start | bytes 4194304 | tf_op jit(solution)/shard_map/psum | solution.py:76
  11.5 78.2 %copy-start = (bf16[1024,1024]{1,0:T(8,128)(2,1)S(1)}, bf16[1024,1024]{1,0:T(8,128)(2,1)}, u32[]{:S(2)}) copy-start(bf16[1024,1024]{1,0:T(8,128)(2,1)} %param.9) | copy-start | bytes 6291460
  55.5 78.4 %copy-start.44 = (bf16[8,64,8,64]{3,2,1,0:T(8,128)(2,1)}, bf16[8,64,8,64]{3,2,1,0:T(8,128)(2,1)S(1)}, u32[]{:S(2)}) copy-start(bf16[8,64,8,64]{3,2,1,0:T(8,128)(2,1)S(1)} %reshape.136) | copy-start | bytes 1572868
  135.8 2.7 copy-start.11
  142.1 28.8 %copy-start.27 = (bf16[512,512]{1,0:T(8,128)(2,1)}, bf16[512,512]{1,0:T(8,128)(2,1)S(1)}, u32[]{:S(2)}) copy-start(bf16[512,512]{1,0:T(8,128)(2,1)S(1)} %reshape.139) | copy-start | bytes 1572868
  170.9 108.2 %all-gather.18.cloned.1.call-start = ((), (), s32[]{:S(2)}) async-start(), calls=%async_computation.13 | async-start | bytes 3063808 | tf_op jit(solution)/shard_map/all_gather | solution.py:146
  171.5 152.5 %all-gather.20.cloned.1.call-start = ((), (), s32[]{:S(2)}) async-start(), calls=%async_computation.14 | async-start | bytes 3063808 | tf_op jit(solution)/shard_map/all_gather | solution.py:147
  172.3 196.7 %all-gather.16.cloned.1.call-start = ((), (), s32[]{:S(2)}) async-start(), calls=%async_computation.12 | async-start | bytes 3063808 | tf_op jit(solution)/shard_map/all_gather | solution.py:145
  173.0 62.2 %copy-start.36 = (bf16[1024,512]{1,0:T(8,128)(2,1)S(1)}, bf16[1024,512]{1,0:T(8,128)(2,1)}, u32[]{:S(2)}) copy-start(bf16[1024,512]{1,0:T(8,128)(2,1)} %all-gather.8.cloned.1.call-done) | copy-start | bytes 3145732
  173.0 315.8 %all-reduce.15.cloned.1.call-start = ((), (), s32[]{:S(2)}) async-start(), calls=%async_computation.24 | async-start | bytes 8388608 | tf_op jit(solution)/shard_map/psum | solution.py:94
  239.1 5.3 copy-start.39
  247.6 3.2 copy-start.46
  251.5 4.4 copy-start.13
  255.9 3.3 copy-start.3
  369.0 7.1 copy-start.54
  376.0 2.9 copy-start.62
  382.1 187.5 %all-reduce.17.cloned.1.call-start = ((), (), s32[]{:S(2)}) async-start(), calls=%async_computation.25 | async-start | bytes 4194304 | tf_op jit(solution)/shard_map/psum | solution.py:90
  488.8 3.7 copy-start.7
  506.4 209.6 %all-reduce.13.cloned.1.call-start = ((), (), s32[]{:S(2)}) async-start(), calls=%async_computation.23 | async-start | bytes 8388608 | tf_op jit(solution)/shard_map/psum | solution.py:94
  506.5 4.2 copy-start.25
  506.5 4.2 copy-start.64
  579.8 2.6 copy-start.12
  579.8 2.8 copy-start.50
  579.8 3.1 copy-start.51
  608.0 209.7 %all-reduce.11.cloned.1.call-start = ((), (), s32[]{:S(2)}) async-start(), calls=%async_computation.15 | async-start | bytes 4194304 | tf_op jit(solution)/shard_map/psum | solution.py:125
  716.1 3.8 copy-start.2
  716.1 4.1 copy-start.8
  716.1 4.7 copy-start.18
  716.1 5.3 copy-start.19
  744.3 6.7 copy-start.32
  748.9 3.0 copy-start.30
  754.5 3.9 copy-start.15
  754.6 149.0 %reduce-scatter.18.cloned.1.call-start = ((), (), s32[]{:S(2)}) async-start(), calls=%async_computation.21 | async-start | bytes 6127616 | tf_op jit(solution)/shard_map/reduce_scatter | solution.py:165
  754.8 3.7 copy-start.26
  762.9 225.6 %reduce-scatter.16.cloned.1.call-start = ((), (), s32[]{:S(2)}) async-start(), calls=%async_computation.20 | async-start | bytes 6127616 | tf_op jit(solution)/shard_map/reduce_scatter | solution.py:164
  763.0 3.6 copy-start.24
  771.1 3.7 copy-start.17
  771.1 302.5 %reduce-scatter.20.cloned.1.call-start = ((), (), s32[]{:S(2)}) async-start(), calls=%async_computation.22 | async-start | bytes 6127616 | tf_op jit(solution)/shard_map/reduce_scatter | solution.py:166
  771.1 3.7 copy-start.21
  779.1 3.5 copy-start.29
  779.1 359.7 %reduce-scatter.14.cloned.1.call-start = ((), (), s32[]{:S(2)}) async-start(), calls=%async_computation.19 | async-start | bytes 2228224 | tf_op jit(solution)/shard_map/reduce_scatter | solution.py:163
  784.8 418.9 %reduce-scatter.12.cloned.1.call-start = ((), (), s32[]{:S(2)}) async-start(), calls=%async_computation.18 | async-start | bytes 2228224 | tf_op jit(solution)/shard_map/reduce_scatter | solution.py:162
  788.9 479.7 %reduce-scatter.10.cloned.1.call-start = ((), (), s32[]{:S(2)}) async-start(), calls=%async_computation.17 | async-start | bytes 2228224 | tf_op jit(solution)/shard_map/reduce_scatter | solution.py:161
  793.0 540.8 %reduce-scatter.8.cloned.1.call-start = ((), (), s32[]{:S(2)}) async-start(), calls=%async_computation.16 | async-start | bytes 2228224 | tf_op jit(solution)/shard_map/reduce_scatter | solution.py:160
  (36 other events, 60.7 us)
Sparse Core Ops, SparseCore 0:
  10.1 40.5 all-gather.7
  52.9 36.8 all-gather.9
  91.9 36.8 all-gather.11
  130.8 36.8 all-gather.13
  171.1 61.9 all-reduce.8
  235.2 43.9 all-gather.17
  281.4 42.5 all-gather.19
  326.3 42.5 all-gather.15
  382.2 106.5 all-reduce.14
  506.6 62.9 all-reduce.16
  608.1 107.9 all-reduce.12
  754.7 62.9 all-reduce.10
  822.1 81.3 reduce-scatter.17
  907.9 80.6 reduce-scatter.15
  992.9 80.6 reduce-scatter.19
  1077.7 61.0 reduce-scatter.13
  1143.0 60.7 reduce-scatter.11
  1207.9 60.6 reduce-scatter.9
  1273.0 60.7 reduce-scatter.7
where the time goes:
time: 1350 us; the launch traced here: 1340 us
  waiting for transfers between devices  1090 us (81%)
  matrix products  135 us (10%)
  local copies, waits for them, and re-layouts  70.3 us (5%)
  other arithmetic  32.1 us (2%)
  between operations  15.3 us (1%)
    psum x2, waiting for transfers between devices, layer_pass(): norm_two_back = lax.psum(two_partial, 'mp')  209 us
    reduce_scatter x1, waiting for transfers between devices, body(): lax.psum_scatter(summed[6], 'dp', scatter_dimension=1, tiled=True)  85 us
    reduce_scatter x1, waiting for transfers between devices, body(): lax.psum_scatter(summed[4], 'dp', scatter_dimension=0, tiled=True)  85 us
    reduce_scatter x1, waiting for transfers between devices, body(): lax.psum_scatter(summed[5], 'dp', scatter_dimension=0, tiled=True)  80 us
    reduce_scatter x1, waiting for transfers between devices, body(): lax.psum_scatter(summed[3], 'dp', scatter_dimension=1, tiled=True)  65.2 us
    reduce_scatter x1, waiting for transfers between devices, body(): lax.psum_scatter(summed[0], 'dp', scatter_dimension=0, tiled=True)  65.1 us
    reduce_scatter x1, waiting for transfers between devices, body(): lax.psum_scatter(summed[2], 'dp', scatter_dimension=0, tiled=True)  64.9 us
    reduce_scatter x1, waiting for transfers between devices, body(): lax.psum_scatter(summed[1], 'dp', scatter_dimension=0, tiled=True)  64.9 us
  transfers between devices with their start and end apart: 19, of which 19 were waited for; matrix products, arithmetic and copies ran while one was open for 9% of the time, Pallas kernels for 0%

commit v1 on v0

--- a/solution.py
+++ b/solution.py
@@ -1,14 +1,829 @@
+import functools
+
 import jax
 import jax.numpy as jnp
 from jax import lax
+from jax.experimental import pallas as pl
+from jax.experimental.pallas import tpu as pltpu
 from jax.sharding import PartitionSpec as P
 
 HEADS = 16
 BLK = 64
 MICRO = 2
 
-
 eps = 1e-06
+
+F32 = jnp.float32
+BF16 = jnp.bfloat16
+MESH = pl.DeviceIdType.MESH
+NZ = 4
+HALF = 128
+WIDE = 256
+ATT_CHUNKS = 4
+ROWS = 64
+
+
+def dot_nn(left, right):
+    return lax.dot_general(left, right, (((1,), (0,)), ((), ())), preferred_element_type=F32)
+
+
+def dot_nt(left, right):
+    return lax.dot_general(left, right, (((1,), (1,)), ((), ())), preferred_element_type=F32)
+
+
+def dot_tn(left, right):
+    return lax.dot_general(left, right, (((0,), (0,)), ((), ())), preferred_element_type=F32)
+
+
+def row_factor(values):
+    return lax.rsqrt(jnp.mean(values * values, axis=-1, keepdims=True) + eps)
+
+
+def layer_kernel(
+    ff_chunks, ff_width,
+    tok_hbm, og_hbm, ash, ssh,
+    bo_hbm, gt_hbm, ga_hbm, gs_hbm,
+    wa, ws, tok, in1, qb, kb, vb, mixed, att, resid, in2, in2t, og, ogt, n2b, b2, hgu,
+    nland, bland, l0s, l1s, l2s, l0a, l1a, l2a, l3a, gout_a, gout_s,
+    loc_sem, a_s, a_r, b_s, b_r, r_s, r_r, q_s, q_r, y_s, y_r, out_sem, credit_s, credit_a,
+):
+    dp = lax.axis_index("dp")
+    y = lax.axis_index("mp")
+    z = lax.div(dp, 4)
+    x = lax.rem(lax.div(dp, 2), 2)
+    c = lax.rem(dp, 2)
+    ox, oy, oc = 1 - x, 1 - y, 1 - c
+
+    def at_dev(zz, xx, cc, yy):
+        return (zz * 4 + xx * 2 + cc, yy)
+
+    dev_x = at_dev(z, ox, c, y)
+    dev_y = at_dev(z, x, c, oy)
+    dev_c = at_dev(z, x, oc, y)
+    z_to = [lax.rem(z + k, NZ) for k in (1, 2, 3)]
+    z_from = [lax.rem(z + NZ - k, NZ) for k in (1, 2, 3)]
+    dev_z = [at_dev(t, x, c, y) for t in z_to]
+
+    def remote(src, dst, ssem, rsem, device):
+        return pltpu.make_async_remote_copy(
+            src_ref=src, dst_ref=dst, send_sem=ssem, recv_sem=rsem,
+            device_id=device, device_id_type=MESH,
+        )
+
+    def send(src, dst, ssem, rsem, device):
+        remote(src, dst, ssem, rsem, device).start()
+
+    def got(dst, ssem, rsem):
+        remote(dst, dst, ssem, rsem, dev_c).wait_recv()
+
+    def sent(src, ssem, rsem):
+        remote(src, src, ssem, rsem, dev_c).wait_send()
+
+    barrier = pltpu.get_barrier_semaphore()
+    for device in [dev_c, dev_x, dev_y] + dev_z:
+        pl.semaphore_signal(barrier, inc=1, device_id=device, device_id_type=MESH)
+
+    own = y * 512
+    peer = oy * 512
+    in_tok = pltpu.make_async_copy(tok_hbm.at[pl.ds(own, 512)], tok, loc_sem.at[0])
+    in_og = pltpu.make_async_copy(og_hbm, og, loc_sem.at[1])
+    in_tok.start()
+    in_og.start()
+    pl.semaphore_wait(barrier, 6)
+
+    ycol = pl.ds(y * HALF, HALF)
+    oycol = pl.ds(oy * HALF, HALF)
+
+    def a_slot(h, zz, xx, cc, col):
+        return wa.at[h, :, zz, xx, cc, :, col]
+
+    allz = slice(None)
+
+    def A1(h):
+        for k in range(3):
+            send(ash.at[h], a_slot(h, z, x, c, ycol), a_s.at[h, k], a_r.at[h, k], dev_z[k])
+        pltpu.make_async_copy(ash.at[h], a_slot(h, z, x, c, ycol), loc_sem.at[2 + h]).start()
+
+    def A2(h):
+        for k in range(3):
+            got(a_slot(h, z_from[k], x, c, ycol), a_s.at[h, k], a_r.at[h, k])
+        pltpu.make_async_copy(ash.at[h], a_slot(h, z, x, c, ycol), loc_sem.at[2 + h]).wait()
+        mine = a_slot(h, allz, x, c, ycol)
+        first, second = (dev_x, dev_y) if h % 2 == 0 else (dev_y, dev_x)
+        send(mine, mine, a_s.at[h, 3], a_r.at[h, 3], first)
+        send(mine, mine, a_s.at[h, 4], a_r.at[h, 4], second)
+        send(mine, mine, a_s.at[h, 6], a_r.at[h, 6], dev_c)
+
+    def a_from_x(h):
+        return a_slot(h, allz, ox, c, ycol)
+
+    def a_from_y(h):
+        return a_slot(h, allz, x, c, oycol)
+
+    def a_first(h):
+        return a_from_x(h) if h % 2 == 0 else a_from_y(h)
+
+    def a_second(h):
+        return a_from_y(h) if h % 2 == 0 else a_from_x(h)
+
+    def a_corner(h):
+        return a_slot(h, allz, ox, c, oycol)
+
+    def A3(h):
+        got(a_first(h), a_s.at[h, 3], a_r.at[h, 3])
+        second = dev_y if h % 2 == 0 else dev_x
+        part = a_first(h)
+        send(part, part, a_s.at[h, 5], a_r.at[h, 5], second)
+        send(part, part, a_s.at[h, 7], a_r.at[h, 7], dev_c)
+
+    def A4(h):
+        got(a_second(h), a_s.at[h, 4], a_r.at[h, 4])
+        part = a_second(h)
+        send(part, part, a_s.at[h, 8], a_r.at[h, 8], dev_c)
+        got(a_corner(h), a_s.at[h, 5], a_r.at[h, 5])
+        part = a_corner(h)
+        send(part, part, a_s.at[h, 9], a_r.at[h, 9], dev_c)
+
+    def A5(h):
+        part = a_slot(h, allz, x, oc, ycol)
+        for k in range(6, 10):
+            got(part, a_s.at[h, k], a_r.at[h, k])
+
+    def a_sent(h):
+        for k in range(3):
+            sent(ash.at[h], a_s.at[h, k], a_r.at[h, k])
+        mine = a_slot(h, allz, x, c, ycol)
+        for k in range(3, 10):
+            sent(mine, a_s.at[h, k], a_r.at[h, k])
+
+    def width(j):
+        return min(WIDE, ff_width - j * WIDE)
+
+    def b_slot(j, zz, xx, cc):
+        return ws.at[j, :, zz, xx, cc, :, pl.ds(0, width(j))]
+
+    def b_shard(j):
+        return ssh.at[j, :, :, pl.ds(0, width(j))]
+
+    def B1(j):
+        for k in range(3):
+            send(b_shard(j), b_slot(j, z, x, c), b_s.at[j, k], b_r.at[j, k], dev_z[k])
+        pltpu.make_async_copy(b_shard(j), b_slot(j, z, x, c), loc_sem.at[2 + ATT_CHUNKS + j]).start()
+
+    def B2(j):
+        for k in range(3):
+            got(b_slot(j, z_from[k], x, c), b_s.at[j, k], b_r.at[j, k])
+        pltpu.make_async_copy(b_shard(j), b_slot(j, z, x, c), loc_sem.at[2 + ATT_CHUNKS + j]).wait()
+        mine = b_slot(j, allz, x, c)
+        send(mine, mine, b_s.at[j, 3], b_r.at[j, 3], dev_x)
+        send(mine, mine, b_s.at[j, 4], b_r.at[j, 4], dev_c)
+
+    def B3(j):
+        part = b_slot(j, allz, ox, c)
+        got(part, b_s.at[j, 3], b_r.at[j, 3])
+        send(part, part, b_s.at[j, 5], b_r.at[j, 5], dev_c)
+
+    def B5(j):
+        got(b_slot(j, allz, x, oc), b_s.at[j, 4], b_r.at[j, 4])
+        got(b_slot(j, allz, ox, oc), b_s.at[j, 5], b_r.at[j, 5])
+
+    def b_sent(j):
+        for k in range(3):
+            sent(b_shard(j), b_s.at[j, k], b_r.at[j, k])
+        for k in range(3, 6):
+            sent(b_slot(j, allz, x, c), b_s.at[j, k], b_r.at[j, k])
+
+    def cols(j):
+        return pl.ds(0, width(j))
+
+    def R1(j):
+        if j >= 2:
+            pl.semaphore_wait(credit_s, 1)
+        send(
+            ws.at[j, :, :, :, oc, :, cols(j)], l0s.at[j % 2, :, :, :, :, cols(j)],
+            r_s.at[j, 0], r_r.at[j, 0], dev_c,
+        )
+
+    def add_into(j, count, into, landing, xx):
+        def body(zz, carry):
+            for k in range(count):
+                total = into[j, k, zz, xx, c].astype(F32) + landing[k, zz].astype(F32)
+                into[j, k, zz, xx, c] = total.astype(BF16)
+            return carry
+
+        lax.fori_loop(0, NZ, body, 0)
+
+    def R2(j):
+        slot = j % 2
+        got(l0s.at[slot, :, :, :, :, cols(j)], r_s.at[j, 0], r_r.at[j, 0])
+        add_into(j, 3, ws, l0s.at[slot, :, :, ox], ox)
+        send(
+            ws.at[j, :, :, ox, c, :, cols(j)], l1s.at[j, :, :, :, cols(j)],
+            r_s.at[j, 1], r_r.at[j, 1], dev_x,
+        )
+        add_into(j, 3, ws, l0s.at[slot, :, :, x], x)
+        if j + 2 < ff_chunks:
+            pl.semaphore_signal(credit_s, inc=1, device_id=dev_c, device_id_type=MESH)
+
+    def R3(j):
+        got(l1s.at[j, :, :, :, cols(j)], r_s.at[j, 1], r_r.at[j, 1])
+        add_into(j, 3, ws, l1s.at[j], x)
+        for k in range(3):
+            send(
+                ws.at[j, :, z_to[k], x, c, :, cols(j)], l2s.at[j, k, :, :, cols(j)],
+                r_s.at[j, 2 + k], r_r.at[j, 2 + k], dev_z[k],
+            )
+
+    def R4(j):
+        for k in range(3):
+            got(l2s.at[j, k, :, :, cols(j)], r_s.at[j, 2 + k], r_r.at[j, 2 + k])
+        for k in range(3):
+            total = ws[j, k, z, x, c].astype(F32)
+            for m in range(3):
+                total = total + l2s[j, m, k].astype(F32)
+            gout_s[j, k] = total
+        pltpu.make_async_copy(gout_s.at[j], gs_hbm.at[j], out_sem.at[j]).start()
+
+    def r_sent(j):
+        sent(ws.at[j, :, :, :, oc, :, cols(j)], r_s.at[j, 0], r_r.at[j, 0])
+        sent(ws.at[j, :, :, ox, c, :, cols(j)], r_s.at[j, 1], r_r.at[j, 1])
+        for k in range(3):
+            sent(ws.at[j, :, z, x, c, :, cols(j)], r_s.at[j, 2 + k], r_r.at[j, 2 + k])
+        pltpu.make_async_copy(gout_s.at[j], gs_hbm.at[j], out_sem.at[j]).wait()
+
+    def Q1(h):
+        if h >= 2:
+            pl.semaphore_wait(credit_a, 1)
+        send(wa.at[h, :, :, :, oc], l0a.at[h % 2], q_s.at[h, 0], q_r.at[h, 0], dev_c)
+
+    def Q2(h):
+        slot = h % 2
+        got(l0a.at[slot], q_s.at[h, 0], q_r.at[h, 0])
+        add_into(h, 4, wa, l0a.at[slot, :, :, ox], ox)
+        send(wa.at[h, :, :, ox, c], l1a.at[h], q_s.at[h, 1], q_r.at[h, 1], dev_x)
+        add_into(h, 4, wa, l0a.at[slot, :, :, x], x)
+        if h + 2 < ATT_CHUNKS:
+            pl.semaphore_signal(credit_a, inc=1, device_id=dev_c, device_id_type=MESH)
+
+    def Q3(h):
+        got(l1a.at[h], q_s.at[h, 1], q_r.at[h, 1])
+        add_into(h, 4, wa, l1a.at[h], x)
+        for k in range(3):
+            send(
+                wa.at[h, :, z_to[k], x, c], l2a.at[h, k],
+                q_s.at[h, 2 + k], q_r.at[h, 2 + k], dev_z[k],
+            )
+
+    def Q4(h):
+        for k in range(3):
+            got(l2a.at[h, k], q_s.at[h, 2 + k], q_r.at[h, 2 + k])
+
+        def total(k, col):
+            result = wa[h, k, z, x, c, :, col].astype(F32)
+            for m in range(3):
+                result = result + l2a[h, m, k, :, col].astype(F32)
+            return result
+
+        for k in range(4):
+            wa[h, k, z, x, c, :, oycol] = total(k, oycol).astype(BF16)
+        send(wa.at[h, :, z, x, c, :, oycol], l3a.at[h], q_s.at[h, 5], q_r.at[h, 5], dev_y)
+        for k in range(4):
+            gout_a[h, k] = total(k, ycol)
+
+    def Q5(h):
+        got(l3a.at[h], q_s.at[h, 5], q_r.at[h, 5])
+        for k in range(4):
+            gout_a[h, k] = gout_a[h, k] + l3a[h, k].astype(F32)
+        pltpu.make_async_copy(gout_a.at[h], ga_hbm.at[h], out_sem.at[ff_chunks + h]).start()
+
+    def q_sent(h):
+        sent(wa.at[h, :, :, :, oc], q_s.at[h, 0], q_r.at[h, 0])
+        sent(wa.at[h, :, :, ox, c], q_s.at[h, 1], q_r.at[h, 1])
+        for k in range(3):
+            sent(wa.at[h, :, z, x, c], q_s.at[h, 2 + k], q_r.at[h, 2 + k])
+        sent(wa.at[h, :, z, x, c, :, oycol], q_s.at[h, 5], q_r.at[h, 5])
+        pltpu.make_async_copy(gout_a.at[h], ga_hbm.at[h], out_sem.at[ff_chunks + h]).wait()
+
+    for h in range(ATT_CHUNKS):
+        A1(h)
+    for j in range(ff_chunks):
+        B1(j)
+
+    lanes = lax.broadcasted_iota(jnp.int32, (HALF, HALF), 1)
+    low_lane = lanes < ROWS
+    half_low = low_lane[:ROWS]
+    rows_i = lax.broadcasted_iota(jnp.int32, (ROWS, HALF), 0)
+    lane_i = lax.broadcasted_iota(jnp.int32, (ROWS, HALF), 1)
+    causal = rows_i <= jnp.where(lane_i < ROWS, lane_i, lane_i - ROWS)
+    zero_b = jnp.zeros((HALF, HALF), BF16)
+    zero_h = jnp.zeros((ROWS, HALF), BF16)
+    scale = float(ROWS) ** (-0.5)
+
+    in_tok.wait()
+
+    def first_norm(i, carry):
+        block = pl.ds(pl.multiple_of(i * 64, 64), 64)
+        values = tok[block, :].astype(F32)
+        in1[block, :] = (values * row_factor(values)).astype(BF16)
+        resid[block, :] = values
+        return carry
+
+    lax.fori_loop(0, 8, first_norm, 0)
+    in_og.wait()
+
+    def clear(i, carry):
+        block = pl.ds(pl.multiple_of(i * 64, 64), 64)
+        n2b[block, :] = jnp.zeros((64, 1024), F32)
+        b2[block, :] = jnp.zeros((64, 1024), F32)
+        return carry
+
+    lax.fori_loop(0, 16, clear, 0)
+    last = ff_chunks - 1
+    if width(last) < WIDE:
+        def clear_pad(i, carry):
+            for k in range(3):
+                for xx in range(2):
+                    for cc in range(2):
+                        ws[last, k, i, xx, cc, :, pl.ds(HALF, HALF)] = zero_h
+            return carry
+
+        lax.fori_loop(0, NZ, clear_pad, 0)
+
+    def transpose_into(dst, src, base, first, count):
+        def body(i, carry):
+            rows = pl.ds(pl.multiple_of(first + i * HALF, HALF), HALF)
+            cols_ = pl.ds(pl.multiple_of(base + i * HALF, HALF), HALF)
+            for n in range(8):
+                dst[pl.ds(n * HALF, HALF), cols_] = src[rows, pl.ds(n * HALF, HALF)].T
+            return carry
+
+        lax.fori_loop(0, count // HALF, body, 0)
+
+    transpose_into(ogt, og, 0, 0, 1024)
+
+    def weight(ref, j, k):
+        return ref[j, k].reshape(1024, WIDE)
+
+    def pair_cols(p):
+        return pl.ds(p * HALF, HALF)
+
+    def spread(top, mask, zero):
+        return jnp.concatenate([jnp.where(mask, top, zero), jnp.where(mask, zero, top)], axis=0)
+
+    def forward_chunk(h):
+        def project(tb, carry):
+            block = pl.ds(pl.multiple_of(tb * WIDE, WIDE), WIDE)
+            left = in1[block, :]
+            qb[h, block, :] = dot_nn(left, weight(wa, h, 0)).astype(BF16)
+            kb[h, block, :] = dot_nn(left, weight(wa, h, 1)).astype(BF16)
+            vb[h, block, :] = dot_nn(left, weight(wa, h, 2)).astype(BF16)
+            return carry
+
+        lax.fori_loop(0, 2, project, 0)
+
+        def unit(g, carry):
+            block = pl.ds(pl.multiple_of(g * HALF, HALF), HALF)
+            for p in range(2):
+                col = pair_cols(p)
+                k2 = spread(kb[h, block, col], low_lane, zero_b)
+                v2 = spread(vb[h, block, col], low_lane, zero_b)
+                st = dot_nt(k2, qb[h, block, col])
+                pieces = []
+                for e in range(2):
+                    raw = jnp.where(half_low, st[e * HALF : e * HALF + ROWS], st[e * HALF + ROWS : (e + 1) * HALF])
+                    score = jnp.where(causal, raw * scale, -1e30)
+                    raised = jnp.exp(score - jnp.max(score, axis=0, keepdims=True))
+                    low = (raised / jnp.sum(raised, axis=0, keepdims=True)).astype(BF16)
+                    att[h, g, p, pl.ds(e * ROWS, ROWS), :] = low
+                    pieces.append(spread(low, half_low, zero_h))
+                pt = jnp.concatenate(pieces, axis=0)
+                mixed[h, block, col] = dot_tn(pt, v2).astype(BF16)
+            return carry
+
+        lax.fori_loop(0, 4, unit, 0)
+
+        def out_project(tb, carry):
+            block = pl.ds(pl.multiple_of(tb * WIDE, WIDE), WIDE)
+            resid[block, :] = resid[block, :] + dot_nt(mixed[h, block, :], weight(wa, h, 3))
+            return carry
+
+        lax.fori_loop(0, 2, out_project, 0)
+
+    def run(table, step, index):
+        for key in sorted(table):
+            def go(key=key):
+                for action, number in table[key]:
+                    action(number)
+            pl.when(index == key)(go)
+
+    A2(0)
+    A2(1)
+    A3(0)
+    A2(2)
+    A3(1)
+    A4(0)
+    A2(3)
+    A3(2)
+    A4(1)
+    A3(3)
+    B2(0)
+    before = {
+        0: [(A5, 0)],
+        1: [(A4, 2), (A5, 1), (B2, 1)],
+        2: [(A4, 3), (A5, 2), (B2, 2)],
+        3: [(A5, 3), (B2, 3)],
+    }
+
+    def attention_step(h, carry):
+        run(before, None, h)
+        forward_chunk(h)
+        return carry
+
+    lax.fori_loop(0, ATT_CHUNKS, attention_step, 0)
+    B3(0)
+
+    def second_norm(i, carry):
+        block = pl.ds(pl.multiple_of(i * 64, 64), 64)
+        values = resid[block, :]
+        in2[pl.ds(pl.multiple_of(own + i * 64, 64), 64), :] = (values * row_factor(values)).astype(BF16)
+        return carry
+
+    def in2_rows(part, owner):
+        return in2.at[pl.ds(owner * 512 + part * 256, 256)]
+
+    for part in range(2):
+        lax.fori_loop(part * 4, part * 4 + 4, second_norm, 0)
+        send(in2_rows(part, y), in2_rows(part, y), y_s.at[part], y_r.at[part], dev_y)
+    transpose_into(in2t, in2, own, own, 512)
+
+    def half_rows(ref, part):
+        return ref.at[pl.ds(part * 256, 256)]
+
+    def nsend(part):
+        return half_rows(in1, part)
+
+    def bsend(part):
+        return in2.at[pl.ds(peer + part * 256, 256)]
+
+    def token_block(j, i):
+        is_last = j == last
+        first = jnp.where(is_last, 2 * oy, 2 * y)
+        index = lax.rem(first + i, 4)
+        block = pl.ds(pl.multiple_of(index * WIDE, WIDE), WIDE)
+        left = in2[block, :]
+        gate = dot_nn(left, weight(ws, j, 0))
+        upper = dot_nn(left, weight(ws, j, 1))
+        hidden_grad = dot_nn(og[block, :], weight(ws, j, 2))
+        hidden = (gate * upper).astype(BF16)
+        gate_back = (hidden_grad * upper).astype(BF16)
+        up_back = (hidden_grad * gate).astype(BF16)
+        hgu[0, block, :] = gate_back
+        hgu[1, block, :] = up_back
+        hgu[2, block, :] = hidden
+        n2b[block, :] = n2b[block, :] + dot_nt(gate_back, weight(ws, j, 0)) + dot_nt(up_back, weight(ws, j, 1))
+        b2[block, :] = b2[block, :] + dot_nt(hidden, weight(ws, j, 2))
+
+        for part in range(2):
+            def ship(part=part):
+                def convert(n, carry):
+                    src = pl.ds(pl.multiple_of(peer + part * 256 + n * 64, 64), 64)
+                    dst = pl.ds(pl.multiple_of(part * 256 + n * 64, 64), 64)
+                    in1[dst, :] = n2b[src, :].astype(BF16)
+                    return carry
+
+                lax.fori_loop(0, 4, convert, 0)
+                send(nsend(part), half_rows(nland, part), y_s.at[2 + part], y_r.at[2 + part], dev_y)
+
+            pl.when(jnp.logical_and(is_last, i == part))(ship)
+
+    def peer_arrives():
+        for part in range(2):
+            got(in2_rows(part, oy), y_s.at[part], y_r.at[part])
+        transpose_into(in2t, in2, peer, peer, 512)
+
+    def gated_body(j, i, carry):
+        pl.when(jnp.logical_and(j == 0, i == 2))(peer_arrives)
+        token_block(j, i)
+        return carry
+
+    def weight_grads(j):
+        def body(r, carry):
+            rows = pl.ds(pl.multiple_of(r * WIDE, WIDE), WIDE)
+            for k, left in ((0, in2t), (1, in2t), (2, ogt)):
+                piece = dot_nn(left[rows, :], hgu[k]).astype(BF16)
+                ws[j, k, r] = piece.reshape(2, 2, ROWS, WIDE)
+            return carry
+
+        lax.fori_loop(0, NZ, body, 0)
+
+    pre, mid, post = {}, {}, {}
+    for j in range(ff_chunks):
+        pre[j] = [(B5, j)]
+        mid[j] = []
+        post[j] = [(R1, j)]
+        if j + ATT_CHUNKS < ff_chunks:
+            pre[j].insert(0, (B2, j + ATT_CHUNKS))
+        if j + 1 < ff_chunks:
+            mid[j].append((B3, j + 1))
+        mid[j].append((b_sent, j))
+        if j >= 1:
+            mid[j].append((R2, j - 1))
+
+    def gated_step(j, carry):
+        run(pre, None, j)
+        lax.fori_loop(0, 4, functools.partial(gated_body, j), 0)
+        run(mid, None, j)
+        weight_grads(j)
+        run(post, None, j)
+        return carry
+
+    lax.fori_loop(0, ff_chunks, gated_step, 0)
+
+    for part in range(2):
+        sent(in2_rows(part, y), y_s.at[part], y_r.at[part])
+    for part in range(2):
+        def convert_b(n, carry, part=part):
+            src = pl.ds(pl.multiple_of(peer + part * 256 + n * 64, 64), 64)
+            in2[src, :] = b2[src, :].astype(BF16)
+            return carry
+
+        lax.fori_loop(0, 4, convert_b, 0)
+        send(bsend(part), half_rows(bland, part), y_s.at[4 + part], y_r.at[4 + part], dev_y)
+    R2(last)
+
+    def first_transposed(i, carry):
+        rows = pl.ds(pl.multiple_of(i * HALF, HALF), HALF)
+        values = tok[rows, :].astype(F32)
+        low = (values * row_factor(values)).astype(BF16)
+        for n in range(8):
+            in2t[pl.ds(n * HALF, HALF), rows] = low[:, n * HALF : (n + 1) * HALF].T
+        return carry
+
+    lax.fori_loop(0, 4, first_transposed, 0)
+
+    for part in range(2):
+        got(half_rows(nland, part), y_s.at[2 + part], y_r.at[2 + part])
+
+    def norm_two_back(i, carry):
+        block = pl.ds(pl.multiple_of(i * 64, 64), 64)
+        mine = pl.ds(pl.multiple_of(own + i * 64, 64), 64)
+        other = pl.ds(pl.multiple_of(peer + i * 64, 64), 64)
+        values = resid[block, :]
+        factor = row_factor(values)
+        normed = values * factor
+        grad = n2b[mine, :] + nland[block, :].astype(F32)
+        back = og[mine, :].astype(F32) + factor * (grad - normed * jnp.mean(grad * normed, axis=-1, keepdims=True))
+        n2b[mine, :] = back
+        n2b[other, :] = jnp.zeros((64, 1024), F32)
+        in2[mine, :] = back.astype(BF16)
+        return carry
+
+    lax.fori_loop(0, 8, norm_two_back, 0)
+    transpose_into(in2t, in2, 512, own, 512)
+
+    for h in range(ATT_CHUNKS):
+        a_sent(h)
+
+    def backward_chunk(h):
+        def project(tb, carry):
+            block = pl.ds(pl.multiple_of(own + tb * WIDE, WIDE), WIDE)
+            hgu[0, pl.ds(pl.multiple_of(512 + tb * WIDE, WIDE), WIDE), :] = dot_nn(
+                in2[block, :], weight(wa, h, 3)
+            ).astype(BF16)
+            return carry
+
+        lax.fori_loop(0, 2, project, 0)
+
+        def unit(g, carry):
+            block = pl.ds(pl.multiple_of(g * HALF, HALF), HALF)
+            for p in range(2):
+                col = pair_cols(p)
+                k2 = spread(kb[h, block, col], low_lane, zero_b)
+                v2 = spread(vb[h, block, col], low_lane, zero_b)
+                back = hgu[0, pl.ds(pl.multiple_of(512 + g * HALF, HALF), HALF), col]
+                grads = dot_nt(v2, back)
+                kept, changed = [], []
+                for e in range(2):
+                    low = att[h, g, p, pl.ds(e * ROWS, ROWS), :]
+                    wide = low.astype(F32)
+                    piece = jnp.where(half_low, grads[e * HALF : e * HALF + ROWS], grads[e * HALF + ROWS : (e + 1) * HALF])
+                    inner = jnp.sum(piece * wide, axis=0, keepdims=True)
+                    changed.append(spread((wide * (piece - inner)).astype(BF16), half_low, zero_h))
+                    kept.append(spread(low, half_low, zero_h))
+                pt = jnp.concatenate(kept, axis=0)
+                dst = jnp.concatenate(changed, axis=0)
+                dv2 = dot_nn(pt, back)
+                dk2 = dot_nn(dst, qb[h, block, col])
+                hgu[0, block, col] = (scale * dot_tn(dst, k2)).astype(BF16)
+                hgu[1, block, col] = (scale * jnp.where(low_lane, dk2[:HALF], dk2[HALF:])).astype(BF16)
+                hgu[2, block, col] = jnp.where(low_lane, dv2[:HALF], dv2[HALF:]).astype(BF16)
+            return carry
+
+        lax.fori_loop(0, 4, unit, 0)
+
+        def input_grads(tb, carry):
+            block = pl.ds(pl.multiple_of(tb * WIDE, WIDE), WIDE)
+            into = pl.ds(pl.multiple_of(peer + tb * WIDE, WIDE), WIDE)
+            total = n2b[into, :]
+            for k in range(3):
+                total = total + dot_nt(hgu[k, block, :], weight(wa, h, k))
+            n2b[into, :] = total
+            return carry
+
+        lax.fori_loop(0, 2, input_grads, 0)
+
+        def weight_part(r, carry):
+            rows = pl.ds(pl.multiple_of(r * WIDE, WIDE), WIDE)
+            left = in2t[rows, pl.ds(0, 512)]
+            for k in range(3):
+                wa[h, k, r] = dot_nn(left, hgu[k, pl.ds(0, 512), :]).astype(BF16).reshape(2, 2, ROWS, WIDE)
+            wa[h, 3, r] = dot_nn(in2t[rows, pl.ds(512, 512)], mixed[h]).astype(BF16).reshape(2, 2, ROWS, WIDE)
+            return carry
+
+        lax.fori_loop(0, NZ, weight_part, 0)
+
+    after = {h: [(Q1, h)] for h in range(ATT_CHUNKS)}
+    for h in range(ATT_CHUNKS):
+        if h >= 1:
+            after[h].append((Q2, h - 1))
+        after[h].append((R3, h))
+        if h >= 1:
+            after[h].append((R4, h - 1))
+
+    def attention_back_step(h, carry):
+        backward_chunk(h)
+        run(after, None, h)
+        return carry
+
+    lax.fori_loop(0, ATT_CHUNKS, attention_back_step, 0)
+
+    for part in range(2):
+        sent(nsend(part), y_s.at[2 + part], y_r.at[2 + part])
+
+    def norm_one_back(i, carry):
+        block = pl.ds(pl.multiple_of(i * 64, 64), 64)
+        mine = pl.ds(pl.multiple_of(own + i * 64, 64), 64)
+        other = pl.ds(pl.multiple_of(peer + i * 64, 64), 64)
+        values = tok[block, :].astype(F32)
+        factor = row_factor(values)
+        normed = values * factor
+        grad = n2b[other, :]
+        back = n2b[mine, :] + factor * (grad - normed * jnp.mean(grad * normed, axis=-1, keepdims=True))
+        in1[block, :] = back.astype(BF16)
+        return carry
+
+    lax.fori_loop(0, 8, norm_one_back, 0)
+    gt_rows = gt_hbm.at[pl.ds(own, 512)]
+    send(in1, gt_rows, y_s.at[6], y_r.at[6], dev_y)
+    keep_gt = pltpu.make_async_copy(in1, gt_rows, loc_sem.at[0])
+    keep_gt.start()
+    Q2(ATT_CHUNKS - 1)
+
+    for part in range(2):
+        got(half_rows(bland, part), y_s.at[4 + part], y_r.at[4 + part])
+
+    def layer_out(i, carry):
+        block = pl.ds(pl.multiple_of(i * 64, 64), 64)
+        mine = pl.ds(pl.multiple_of(own + i * 64, 64), 64)
+        nland[block, :] = (resid[block, :] + (b2[mine, :] + bland[block, :].astype(F32))).astype(BF16)
+        return carry
+
+    lax.fori_loop(0, 8, layer_out, 0)
+    bo_rows = bo_hbm.at[pl.ds(own, 512)]
+    send(nland, bo_rows, y_s.at[7], y_r.at[7], dev_y)
+    keep_bo = pltpu.make_async_copy(nland, bo_rows, loc_sem.at[1])
+    keep_bo.start()
+
+    for j in range(ATT_CHUNKS, ff_chunks):
+        R3(j)
+    for j in range(ATT_CHUNKS - 1, ff_chunks):
+        R4(j)
+    Q3(0)
+    Q3(1)
+    Q4(0)
+    Q3(2)
+    Q4(1)
+    Q5(0)
+    Q3(3)
+    Q4(2)
+    Q5(1)
+    Q4(3)
+    Q5(2)
+    Q5(3)
+
+    for part in range(2):
+        sent(bsend(part), y_s.at[4 + part], y_r.at[4 + part])
+    sent(in1, y_s.at[6], y_r.at[6])
+    sent(nland, y_s.at[7], y_r.at[7])
+    got(gt_hbm.at[pl.ds(peer, 512)], y_s.at[6], y_r.at[6])
+    got(bo_hbm.at[pl.ds(peer, 512)], y_s.at[7], y_r.at[7])
+    keep_gt.wait()
+    keep_bo.wait()
+    for j in range(ff_chunks):
+        r_sent(j)
+    for h in range(ATT_CHUNKS):
+        q_sent(h)
+
+
+def fast_body(ff_chunks, ff_width, tokens, w_query, w_key, w_value, w_out, w_gate, w_up, w_down, out_grad):
+    def attention_shard(matrix):
+        return matrix.reshape(ROWS, ATT_CHUNKS, HALF).transpose(1, 0, 2)
+
+    def gated_shard(matrix):
+        padded = jnp.pad(matrix, ((0, 0), (0, ff_chunks * WIDE - ff_width)))
+        return padded.reshape(ROWS, ff_chunks, WIDE).transpose(1, 0, 2)
+
+    ash = jnp.stack([attention_shard(w) for w in (w_query, w_key, w_value, w_out.T)], axis=1)
+    ssh = jnp.stack([gated_shard(w) for w in (w_gate, w_up, w_down.T)], axis=1)
+    count, width = tokens.shape
+    half = count // 2
+    vm = pltpu.VMEM
+    dma = pltpu.SemaphoreType.DMA
+    scratch = [
+        vm((ATT_CHUNKS, 4, NZ, 2, 2, ROWS, WIDE), BF16),
+        vm((ff_chunks, 3, NZ, 2, 2, ROWS, WIDE), BF16),
+        vm((half, width), BF16),
+        vm((half, width), BF16),
+        vm((ATT_CHUNKS, half, WIDE), BF16),
+        vm((ATT_CHUNKS, half, WIDE), BF16),
+        vm((ATT_CHUNKS, half, WIDE), BF16),
+        vm((ATT_CHUNKS, half, WIDE), BF16),
+        vm((ATT_CHUNKS, 4, 2, HALF, HALF), BF16),
+        vm((half, width), F32),
+        vm((count, width), BF16),
+        vm((width, count), BF16),
+        vm((count, width), BF16),
+        vm((width, count), BF16),
+        vm((count, width), F32),
+        vm((count, width), F32),
+        vm((3, count, WIDE), BF16),
+        vm((half, width), BF16),
+        vm((half, width), BF16),
+        vm((2, 3, NZ, 2, ROWS, WIDE), BF16),
+        vm((ff_chunks, 3, NZ, ROWS, WIDE), BF16),
+        vm((ff_chunks, 3, 3, ROWS, WIDE), BF16),
+        vm((2, 4, NZ, 2, ROWS, WIDE), BF16),
+        vm((ATT_CHUNKS, 4, NZ, ROWS, WIDE), BF16),
+        vm((ATT_CHUNKS, 3, 4, ROWS, WIDE), BF16),
+        vm((ATT_CHUNKS, 4, ROWS, HALF), BF16),
+        vm((ATT_CHUNKS, 4, ROWS, HALF), F32),
+        vm((ff_chunks, 3, ROWS, WIDE), F32),
+        dma((2 + ATT_CHUNKS + ff_chunks,)),
+        dma((ATT_CHUNKS, 10)),
+        dma((ATT_CHUNKS, 10)),
+        dma((ff_chunks, 6)),
+        dma((ff_chunks, 6)),
+        dma((ff_chunks, 5)),
+        dma((ff_chunks, 5)),
+        dma((ATT_CHUNKS, 6)),
+        dma((ATT_CHUNKS, 6)),
+        dma((8,)),
+        dma((8,)),
+        dma((ff_chunks + ATT_CHUNKS,)),
+        pltpu.SemaphoreType.REGULAR,
+        pltpu.SemaphoreType.REGULAR,
+    ]
+    anywhere = pl.BlockSpec(memory_space=pl.ANY)
+    block_out, grad_tokens, ga, gs = pl.pallas_call(
+        functools.partial(layer_kernel, ff_chunks, ff_width),
+        out_shape=(
+            jax.ShapeDtypeStruct((count, width), BF16),
+            jax.ShapeDtypeStruct((count, width), BF16),
+            jax.ShapeDtypeStruct((ATT_CHUNKS, 4, ROWS, HALF), F32),
+            jax.ShapeDtypeStruct((ff_chunks, 3, ROWS, WIDE), F32),
+        ),
+        in_specs=[anywhere] * 4,
+        out_specs=(anywhere,) * 4,
+        scratch_shapes=scratch,
+        compiler_params=pltpu.CompilerParams(
+            collective_id=0, has_side_effects=True, vmem_limit_bytes=67043328
+        ),
+        name="layer",
+    )(tokens, out_grad, ash, ssh)
+
+    def attention_grad(k):
+        return ga[:, k].transpose(1, 0, 2).reshape(ROWS, ATT_CHUNKS * HALF)
+
+    def gated_grad(k):
+        return gs[:, k].transpose(1, 0, 2).reshape(ROWS, ff_chunks * WIDE)[:, :ff_width]
+
+    return (
+        block_out, grad_tokens, attention_grad(0), attention_grad(1), attention_grad(2),
+        attention_grad(3).T, gated_grad(0), gated_grad(1), gated_grad(2).T,
+    )
+
+
+def fits(mesh, shapes):
+    sizes = dict(mesh.shape)
+    tokens, w_query, w_gate = shapes[0], shapes[1], shapes[5]
+    return (
+        sizes.get("dp") == 16
+        and sizes.get("mp") == 2
+        and tokens == (16384, 1024)
+        and w_query == (1024, 1024)
+        and w_gate[1] % (2 * HALF) == 0
+        and w_gate[1] // 2 <= 6 * WIDE
+    )
 
 
 def normalize(values_in):
@@ -201,4 +1016,16 @@
         P("dp", "mp"),
         P("mp", "dp"),
     )
-    return jax.shard_map(body, mesh=mesh, in_specs=in_specs, out_specs=out_specs, check_vma=False)
+
+    def program(*args):
+        shapes = [a.shape for a in args]
+        if fits(mesh, shapes):
+            ff_width = shapes[5][1] // 2
+            chosen = functools.partial(fast_body, pl.cdiv(ff_width, WIDE), ff_width)
+        else:
+            chosen = body
+        return jax.shard_map(
+            chosen, mesh=mesh, in_specs=in_specs, out_specs=out_specs, check_vma=False
+        )(*args)
+
+    return program

time: 1350 us -> 286 us (0.21)
  waiting for transfers between devices: 1090 us -> 0 us
  Pallas kernels: 0 us -> 268 us
  matrix products: 135 us -> 0 us
  local copies, waits for them, and re-layouts: 70.3 us -> 13.8 us
  other arithmetic: 32.1 us -> 1.62 us
  between operations: 15.3 us -> 0.76 us
    reduce_scatter x7 -> x0, waiting for transfers between devices: 510 us -> none  [the longest x1 85 us: body(): lax.psum_scatter(summed[6], 'dp', scatter_dimension=1, tiled=True)]
    psum x5 -> x0, waiting for transfers between devices: 341 us -> none  [the longest x2 209 us: layer_pass(): norm_two_back = lax.psum(two_partial, 'mp')]
    pallas_call x0 -> x1, Pallas kernels: none -> 268 us  [fast_body(): pl.pallas_call(functools.partial(layer_kernel, ff_chunks, ff_width), out_...]
    all_gather x7 -> x0, waiting for transfers between devices: 230 us -> none  [the longest x1 39.4 us: body(): lax.all_gather(w_down, 'dp', axis=1, tiled=True)]
    dot_general x54 -> x0, matrix products: 135 us -> none  [the longest x14 45.1 us: forward_product(): return jnp.dot(left, right, preferred_element_type=jnp.float32)]
    reshape x16 -> x8, local copies, waits for them, and re-layouts: 35.8 us -> 2.75 us  [the longest x4 2.66 us: attention_grad(): return ga[:, k].transpose(1, 0, 2).reshape(ROWS, ATT_CHUNKS * HALF)]
    convert_element_type x8 -> x0, local copies, waits for them, and re-layouts: 15.7 us -> none  [the longest x2 4.99 us: layer_pass(): query_back = join_heads(query_back.astype(jnp.bfloat16))]
    reduce_sum x7 -> x0, other arithmetic: 14.4 us -> none  [the longest x3 9.63 us: norm_back(): jnp.mean(grad_normed * normed, axis=-1, keepdims=True)]
  transfers between devices with their start and end apart: 19 -> 0, of which waited for: 19 -> 0; matrix products, arithmetic and copies ran while one was open for 9% -> 0% of each run, Pallas kernels for 0% -> 0%
where the time goes in v1:
time: 286 us; the launch traced here: 284 us
  Pallas kernels  268 us (94%)
  local copies, waits for them, and re-layouts  13.8 us (5%)
    pallas_call x1, Pallas kernels, fast_body(): pl.pallas_call(functools.partial(layer_kernel, ff_chunks, ff_width), out_...  268 us

profile of v1, /device:TPU:0, one launch (start us, length us, event | category | flops | bytes accessed | tf_op | source)
XLA Modules:
  0.0 283.9 jit_solution(17072666822285233875)
XLA Ops:
  0.6 0.0 copy-start.3
  0.7 0.9 bitcast_bitcast_fusion.4
  1.6 0.9 bitcast_bitcast_fusion.6
  2.5 0.7 pad_maximum_fusion.1.ash
  3.2 0.9 pad.11
  4.2 0.9 pad.12
  5.2 0.0 copy-done.3
  5.2 0.9 pad_maximum_fusion.ssh
  6.1 267.7 %layer.1 = (bf16[1024,1024]{1,0:T(8,128)(2,1)}, bf16[1024,1024]{1,0:T(8,128)(2,1)}, f32[4,4,64,128]{3,2,1,0:T(8,128)}, f32[6,3,64,256]{3,2,1,0:T(8,128)}) custom-call(bf16[1024,1024]{1,0:T(8,128)(2,1)} %tok_hbm.1, bf16[1024,1024]{1,0:T(8,128)(2,1)} %og_hbm.1, bf16[4,4,64,128]{3,2,1,0:T(8,128)(2,1)} %pad_maximum_fusion.1.ash, ...), custom_call_target="tpu_custom_call" | custom-call | tf_op jit(solution)/shard_map/layer/pallas_call | solution.py:787
  273.8 0.0 copy-start.2
  273.8 1.2 slice_bitcast_fusion.4
  275.1 0.7 copy.58
  275.8 0.7 copy.59
  276.4 0.7 copy.60
  277.1 0.7 copy.61
  277.7 0.0 copy-done.2
  277.7 0.1 slice_bitcast_fusion
  277.8 0.0 copy-start.1
  277.9 0.8 slice.40
  278.7 0.8 slice.41
  279.5 0.8 slice_bitcast_fusion.3
  280.2 0.0 copy-done.1
  280.2 0.0 copy-start
  280.2 1.3 copy.64
  281.6 1.0 copy-done
  282.6 1.3 copy.65
  (6 shorter events, 0.1 us)
Async XLA Ops:
  0.6 4.5 %copy-start.3 = (bf16[64,1408]{1,0:T(8,128)(2,1)S(1)}, bf16[64,1408]{1,0:T(8,128)(2,1)}, u32[]{:S(2)}) copy-start(bf16[64,1408]{1,0:T(8,128)(2,1)} %param.14) | copy-start | bytes 540676
  273.8 3.9 %copy-start.2 = (f32[6,3,64,256]{3,2,1,0:T(8,128)S(1)}, f32[6,3,64,256]{3,2,1,0:T(8,128)}, u32[]{:S(2)}) copy-start(f32[6,3,64,256]{3,2,1,0:T(8,128)} %get-tuple-element.16) | copy-start | bytes 3538948
  277.8 2.4 copy-start.1
  280.2 2.3 copy-start

commit v2 on v1

--- a/solution.py
+++ b/solution.py
@@ -43,9 +43,9 @@
     ff_chunks, ff_width,
     tok_hbm, og_hbm, ash, ssh,
     bo_hbm, gt_hbm, ga_hbm, gs_hbm,
-    wa, ws, tok, in1, qb, kb, vb, mixed, att, resid, in2, in2t, og, ogt, n2b, b2, hgu,
-    nland, bland, l0s, l1s, l2s, l0a, l1a, l2a, l3a, gout_a, gout_s,
-    loc_sem, a_s, a_r, b_s, b_r, r_s, r_r, q_s, q_r, y_s, y_r, out_sem, credit_s, credit_a,
+    wa, ws, tok, in1, qb, kb, vb, mixed, att, resid, in2, in2t, og, ogt, nown, bown, pacc, hgu,
+    nland, bland, l0, l1s, l2s, l1a, l2a, l3a, gout_a, gout_s,
+    loc_sem, a_s, a_r, b_s, b_r, r_s, r_r, q_s, q_r, y_s, y_r, out_sem, credit,
 ):
     dp = lax.axis_index("dp")
     y = lax.axis_index("mp")
@@ -198,9 +198,9 @@
 
     def R1(j):
         if j >= 2:
-            pl.semaphore_wait(credit_s, 1)
+            pl.semaphore_wait(credit, 1)
         send(
-            ws.at[j, :, :, :, oc, :, cols(j)], l0s.at[j % 2, :, :, :, :, cols(j)],
+            ws.at[j, :, :, :, oc, :, cols(j)], l0.at[j % 2, pl.ds(0, 3), :, :, :, cols(j)],
             r_s.at[j, 0], r_r.at[j, 0], dev_c,
         )
 
@@ -215,15 +215,15 @@
 
     def R2(j):
         slot = j % 2
-        got(l0s.at[slot, :, :, :, :, cols(j)], r_s.at[j, 0], r_r.at[j, 0])
-        add_into(j, 3, ws, l0s.at[slot, :, :, ox], ox)
+        got(l0.at[slot, pl.ds(0, 3), :, :, :, cols(j)], r_s.at[j, 0], r_r.at[j, 0])
+        add_into(j, 3, ws, l0.at[slot, :, :, ox], ox)
         send(
             ws.at[j, :, :, ox, c, :, cols(j)], l1s.at[j, :, :, :, cols(j)],
             r_s.at[j, 1], r_r.at[j, 1], dev_x,
         )
-        add_into(j, 3, ws, l0s.at[slot, :, :, x], x)
-        if j + 2 < ff_chunks:
-            pl.semaphore_signal(credit_s, inc=1, device_id=dev_c, device_id_type=MESH)
+        add_into(j, 3, ws, l0.at[slot, :, :, x], x)
+        if j + 2 < ff_chunks + ATT_CHUNKS:
+            pl.semaphore_signal(credit, inc=1, device_id=dev_c, device_id_type=MESH)
 
     def R3(j):
         got(l1s.at[j, :, :, :, cols(j)], r_s.at[j, 1], r_r.at[j, 1])
@@ -252,18 +252,18 @@
         pltpu.make_async_copy(gout_s.at[j], gs_hbm.at[j], out_sem.at[j]).wait()
 
     def Q1(h):
-        if h >= 2:
-            pl.semaphore_wait(credit_a, 1)
-        send(wa.at[h, :, :, :, oc], l0a.at[h % 2], q_s.at[h, 0], q_r.at[h, 0], dev_c)
+        if ff_chunks + h >= 2:
+            pl.semaphore_wait(credit, 1)
+        send(wa.at[h, :, :, :, oc], l0.at[(ff_chunks + h) % 2], q_s.at[h, 0], q_r.at[h, 0], dev_c)
 
     def Q2(h):
-        slot = h % 2
-        got(l0a.at[slot], q_s.at[h, 0], q_r.at[h, 0])
-        add_into(h, 4, wa, l0a.at[slot, :, :, ox], ox)
+        slot = (ff_chunks + h) % 2
+        got(l0.at[slot], q_s.at[h, 0], q_r.at[h, 0])
+        add_into(h, 4, wa, l0.at[slot, :, :, ox], ox)
         send(wa.at[h, :, :, ox, c], l1a.at[h], q_s.at[h, 1], q_r.at[h, 1], dev_x)
-        add_into(h, 4, wa, l0a.at[slot, :, :, x], x)
+        add_into(h, 4, wa, l0.at[slot, :, :, x], x)
         if h + 2 < ATT_CHUNKS:
-            pl.semaphore_signal(credit_a, inc=1, device_id=dev_c, device_id_type=MESH)
+            pl.semaphore_signal(credit, inc=1, device_id=dev_c, device_id_type=MESH)
 
     def Q3(h):
         got(l1a.at[h], q_s.at[h, 1], q_r.at[h, 1])
@@ -306,8 +306,6 @@
 
     for h in range(ATT_CHUNKS):
         A1(h)
-    for j in range(ff_chunks):
-        B1(j)
 
     lanes = lax.broadcasted_iota(jnp.int32, (HALF, HALF), 1)
     low_lane = lanes < ROWS
@@ -329,25 +327,20 @@
         return carry
 
     lax.fori_loop(0, 8, first_norm, 0)
-    in_og.wait()
-
     def clear(i, carry):
         block = pl.ds(pl.multiple_of(i * 64, 64), 64)
-        n2b[block, :] = jnp.zeros((64, 1024), F32)
-        b2[block, :] = jnp.zeros((64, 1024), F32)
-        return carry
-
-    lax.fori_loop(0, 16, clear, 0)
+        nown[block, :] = jnp.zeros((64, 1024), F32)
+        bown[block, :] = jnp.zeros((64, 1024), F32)
+        return carry
+
     last = ff_chunks - 1
-    if width(last) < WIDE:
-        def clear_pad(i, carry):
-            for k in range(3):
-                for xx in range(2):
-                    for cc in range(2):
-                        ws[last, k, i, xx, cc, :, pl.ds(HALF, HALF)] = zero_h
-            return carry
-
-        lax.fori_loop(0, NZ, clear_pad, 0)
+
+    def clear_pad(i, carry):
+        for k in range(3):
+            for xx in range(2):
+                for cc in range(2):
+                    ws[last, k, i, xx, cc, :, pl.ds(HALF, HALF)] = zero_h
+        return carry
 
     def transpose_into(dst, src, base, first, count):
         def body(i, carry):
@@ -358,8 +351,6 @@
             return carry
 
         lax.fori_loop(0, count // HALF, body, 0)
-
-    transpose_into(ogt, og, 0, 0, 1024)
 
     def weight(ref, j, k):
         return ref[j, k].reshape(1024, WIDE)
@@ -417,14 +408,22 @@
             pl.when(index == key)(go)
 
     A2(0)
+    for j in range(ff_chunks):
+        B1(j)
     A2(1)
     A3(0)
+    lax.fori_loop(0, 8, clear, 0)
+    if width(last) < WIDE:
+        lax.fori_loop(0, NZ, clear_pad, 0)
     A2(2)
     A3(1)
     A4(0)
+    in_og.wait()
+    transpose_into(ogt, og, 0, 0, 512)
     A2(3)
     A3(2)
     A4(1)
+    transpose_into(ogt, og, 512, 512, 512)
     A3(3)
     B2(0)
     before = {
@@ -465,11 +464,7 @@
     def bsend(part):
         return in2.at[pl.ds(peer + part * 256, 256)]
 
-    def token_block(j, i):
-        is_last = j == last
-        first = jnp.where(is_last, 2 * oy, 2 * y)
-        index = lax.rem(first + i, 4)
-        block = pl.ds(pl.multiple_of(index * WIDE, WIDE), WIDE)
+    def gated_block(j, block):
         left = in2[block, :]
         gate = dot_nn(left, weight(ws, j, 0))
         upper = dot_nn(left, weight(ws, j, 1))
@@ -477,44 +472,11 @@
         hidden = (gate * upper).astype(BF16)
         gate_back = (hidden_grad * upper).astype(BF16)
         up_back = (hidden_grad * gate).astype(BF16)
-        hgu[0, block, :] = gate_back
-        hgu[1, block, :] = up_back
-        hgu[2, block, :] = hidden
-        n2b[block, :] = n2b[block, :] + dot_nt(gate_back, weight(ws, j, 0)) + dot_nt(up_back, weight(ws, j, 1))
-        b2[block, :] = b2[block, :] + dot_nt(hidden, weight(ws, j, 2))
-
-        for part in range(2):
-            def ship(part=part):
-                def convert(n, carry):
-                    src = pl.ds(pl.multiple_of(peer + part * 256 + n * 64, 64), 64)
-                    dst = pl.ds(pl.multiple_of(part * 256 + n * 64, 64), 64)
-                    in1[dst, :] = n2b[src, :].astype(BF16)
-                    return carry
-
-                lax.fori_loop(0, 4, convert, 0)
-                send(nsend(part), half_rows(nland, part), y_s.at[2 + part], y_r.at[2 + part], dev_y)
-
-            pl.when(jnp.logical_and(is_last, i == part))(ship)
-
-    def peer_arrives():
-        for part in range(2):
-            got(in2_rows(part, oy), y_s.at[part], y_r.at[part])
-        transpose_into(in2t, in2, peer, peer, 512)
-
-    def gated_body(j, i, carry):
-        pl.when(jnp.logical_and(j == 0, i == 2))(peer_arrives)
-        token_block(j, i)
-        return carry
-
-    def weight_grads(j):
-        def body(r, carry):
-            rows = pl.ds(pl.multiple_of(r * WIDE, WIDE), WIDE)
-            for k, left in ((0, in2t), (1, in2t), (2, ogt)):
-                piece = dot_nn(left[rows, :], hgu[k]).astype(BF16)
-                ws[j, k, r] = piece.reshape(2, 2, ROWS, WIDE)
-            return carry
-
-        lax.fori_loop(0, NZ, body, 0)
+        hgu[0, j, block, :] = gate_back
+        hgu[1, j, block, :] = up_back
+        hgu[2, j, block, :] = hidden
+        norm_part = dot_nt(gate_back, weight(ws, j, 0)) + dot_nt(up_back, weight(ws, j, 1))
+        return norm_part, dot_nt(hidden, weight(ws, j, 2))
 
     pre, mid, post = {}, {}, {}
     for j in range(ff_chunks):
@@ -525,30 +487,85 @@
             pre[j].insert(0, (B2, j + ATT_CHUNKS))
         if j + 1 < ff_chunks:
             mid[j].append((B3, j + 1))
-        mid[j].append((b_sent, j))
         if j >= 1:
-            mid[j].append((R2, j - 1))
-
-    def gated_step(j, carry):
+            post[j].append((R2, j - 1))
+
+    def own_pass(j, carry):
         run(pre, None, j)
-        lax.fori_loop(0, 4, functools.partial(gated_body, j), 0)
+
+        def body(i, inner):
+            rows = pl.ds(pl.multiple_of(i * WIDE, WIDE), WIDE)
+            norm_part, branch_part = gated_block(j, pl.ds(pl.multiple_of(own + i * WIDE, WIDE), WIDE))
+            nown[rows, :] = nown[rows, :] + norm_part
+            bown[rows, :] = bown[rows, :] + branch_part
+            return inner
+
+        lax.fori_loop(0, 2, body, 0)
         run(mid, None, j)
+        return carry
+
+    lax.fori_loop(0, ff_chunks, own_pass, 0)
+
+    def peer_pass(part, carry):
+        got(in2_rows(part, oy), y_s.at[part], y_r.at[part])
+        block = pl.ds(pl.multiple_of(peer + part * WIDE, WIDE), WIDE)
+
+        def zero(n, inner):
+            rows = pl.ds(pl.multiple_of(n * 64, 64), 64)
+            pacc[0, rows, :] = jnp.zeros((64, 1024), F32)
+            pacc[1, rows, :] = jnp.zeros((64, 1024), F32)
+            return inner
+
+        lax.fori_loop(0, 4, zero, 0)
+
+        def body(j, inner):
+            norm_part, branch_part = gated_block(j, block)
+            pacc[0] = pacc[0] + norm_part
+            pacc[1] = pacc[1] + branch_part
+            return inner
+
+        lax.fori_loop(0, ff_chunks, body, 0)
+
+        def convert(n, inner):
+            src = pl.ds(pl.multiple_of(n * 64, 64), 64)
+            in1[pl.ds(pl.multiple_of(part * WIDE + n * 64, 64), 64), :] = pacc[0, src, :].astype(BF16)
+            return inner
+
+        lax.fori_loop(0, 4, convert, 0)
+        send(nsend(part), half_rows(nland, part), y_s.at[2 + part], y_r.at[2 + part], dev_y)
+        transpose_into(in2t, in2, peer + part * WIDE, peer + part * WIDE, WIDE)
+
+        def convert_b(n, inner):
+            src = pl.ds(pl.multiple_of(n * 64, 64), 64)
+            in2[pl.ds(pl.multiple_of(peer + part * WIDE + n * 64, 64), 64), :] = pacc[1, src, :].astype(BF16)
+            return inner
+
+        lax.fori_loop(0, 4, convert_b, 0)
+        return carry
+
+    lax.fori_loop(0, 2, peer_pass, 0)
+    for part in range(2):
+        send(bsend(part), half_rows(bland, part), y_s.at[4 + part], y_r.at[4 + part], dev_y)
+        sent(in2_rows(part, y), y_s.at[part], y_r.at[part])
+    for j in range(ff_chunks):
+        b_sent(j)
+
+    def weight_grads(j):
+        def body(r, carry):
+            rows = pl.ds(pl.multiple_of(r * WIDE, WIDE), WIDE)
+            for k, left in ((0, in2t), (1, in2t), (2, ogt)):
+                piece = dot_nn(left[rows, :], hgu[k, j]).astype(BF16)
+                ws[j, k, r] = piece.reshape(2, 2, ROWS, WIDE)
+            return carry
+
+        lax.fori_loop(0, NZ, body, 0)
+
+    def grads_step(j, carry):
         weight_grads(j)
         run(post, None, j)
         return carry
 
-    lax.fori_loop(0, ff_chunks, gated_step, 0)
-
-    for part in range(2):
-        sent(in2_rows(part, y), y_s.at[part], y_r.at[part])
-    for part in range(2):
-        def convert_b(n, carry, part=part):
-            src = pl.ds(pl.multiple_of(peer + part * 256 + n * 64, 64), 64)
-            in2[src, :] = b2[src, :].astype(BF16)
-            return carry
-
-        lax.fori_loop(0, 4, convert_b, 0)
-        send(bsend(part), half_rows(bland, part), y_s.at[4 + part], y_r.at[4 + part], dev_y)
+    lax.fori_loop(0, ff_chunks, grads_step, 0)
     R2(last)
 
     def first_transposed(i, carry):
@@ -567,18 +584,24 @@
     def norm_two_back(i, carry):
         block = pl.ds(pl.multiple_of(i * 64, 64), 64)
         mine = pl.ds(pl.multiple_of(own + i * 64, 64), 64)
-        other = pl.ds(pl.multiple_of(peer + i * 64, 64), 64)
         values = resid[block, :]
         factor = row_factor(values)
         normed = values * factor
-        grad = n2b[mine, :] + nland[block, :].astype(F32)
+        grad = nown[block, :] + nland[block, :].astype(F32)
         back = og[mine, :].astype(F32) + factor * (grad - normed * jnp.mean(grad * normed, axis=-1, keepdims=True))
-        n2b[mine, :] = back
-        n2b[other, :] = jnp.zeros((64, 1024), F32)
+        nown[block, :] = back
         in2[mine, :] = back.astype(BF16)
         return carry
 
     lax.fori_loop(0, 8, norm_two_back, 0)
+
+    def zero_acc(n, carry):
+        rows = pl.ds(pl.multiple_of(n * 64, 64), 64)
+        for part in range(2):
+            pacc[part, rows, :] = jnp.zeros((64, 1024), F32)
+        return carry
+
+    lax.fori_loop(0, 4, zero_acc, 0)
     transpose_into(in2t, in2, 512, own, 512)
 
     for h in range(ATT_CHUNKS):
@@ -587,7 +610,7 @@
     def backward_chunk(h):
         def project(tb, carry):
             block = pl.ds(pl.multiple_of(own + tb * WIDE, WIDE), WIDE)
-            hgu[0, pl.ds(pl.multiple_of(512 + tb * WIDE, WIDE), WIDE), :] = dot_nn(
+            hgu[0, 0, pl.ds(pl.multiple_of(512 + tb * WIDE, WIDE), WIDE), :] = dot_nn(
                 in2[block, :], weight(wa, h, 3)
             ).astype(BF16)
             return carry
@@ -600,7 +623,7 @@
                 col = pair_cols(p)
                 k2 = spread(kb[h, block, col], low_lane, zero_b)
                 v2 = spread(vb[h, block, col], low_lane, zero_b)
-                back = hgu[0, pl.ds(pl.multiple_of(512 + g * HALF, HALF), HALF), col]
+                back = hgu[0, 0, pl.ds(pl.multiple_of(512 + g * HALF, HALF), HALF), col]
                 grads = dot_nt(v2, back)
                 kept, changed = [], []
                 for e in range(2):
@@ -614,20 +637,19 @@
                 dst = jnp.concatenate(changed, axis=0)
                 dv2 = dot_nn(pt, back)
                 dk2 = dot_nn(dst, qb[h, block, col])
-                hgu[0, block, col] = (scale * dot_tn(dst, k2)).astype(BF16)
-                hgu[1, block, col] = (scale * jnp.where(low_lane, dk2[:HALF], dk2[HALF:])).astype(BF16)
-                hgu[2, block, col] = jnp.where(low_lane, dv2[:HALF], dv2[HALF:]).astype(BF16)
+                hgu[0, 0, block, col] = (scale * dot_tn(dst, k2)).astype(BF16)
+                hgu[1, 0, block, col] = (scale * jnp.where(low_lane, dk2[:HALF], dk2[HALF:])).astype(BF16)
+                hgu[2, 0, block, col] = jnp.where(low_lane, dv2[:HALF], dv2[HALF:]).astype(BF16)
             return carry
 
         lax.fori_loop(0, 4, unit, 0)
 
         def input_grads(tb, carry):
             block = pl.ds(pl.multiple_of(tb * WIDE, WIDE), WIDE)
-            into = pl.ds(pl.multiple_of(peer + tb * WIDE, WIDE), WIDE)
-            total = n2b[into, :]
+            total = pacc[tb]
             for k in range(3):
-                total = total + dot_nt(hgu[k, block, :], weight(wa, h, k))
-            n2b[into, :] = total
+                total = total + dot_nt(hgu[k, 0, block, :], weight(wa, h, k))
+            pacc[tb] = total
             return carry
 
         lax.fori_loop(0, 2, input_grads, 0)
@@ -636,19 +658,34 @@
             rows = pl.ds(pl.multiple_of(r * WIDE, WIDE), WIDE)
             left = in2t[rows, pl.ds(0, 512)]
             for k in range(3):
-                wa[h, k, r] = dot_nn(left, hgu[k, pl.ds(0, 512), :]).astype(BF16).reshape(2, 2, ROWS, WIDE)
+                wa[h, k, r] = dot_nn(left, hgu[k, 0, pl.ds(0, 512), :]).astype(BF16).reshape(2, 2, ROWS, WIDE)
             wa[h, 3, r] = dot_nn(in2t[rows, pl.ds(512, 512)], mixed[h]).astype(BF16).reshape(2, 2, ROWS, WIDE)
             return carry
 
         lax.fori_loop(0, NZ, weight_part, 0)
 
-    after = {h: [(Q1, h)] for h in range(ATT_CHUNKS)}
-    for h in range(ATT_CHUNKS):
-        if h >= 1:
-            after[h].append((Q2, h - 1))
-        after[h].append((R3, h))
-        if h >= 1:
-            after[h].append((R4, h - 1))
+    bo_rows = bo_hbm.at[pl.ds(own, 512)]
+
+    def emit_out(_):
+        for part in range(2):
+            got(half_rows(bland, part), y_s.at[4 + part], y_r.at[4 + part])
+
+        def layer_out(i, carry):
+            block = pl.ds(pl.multiple_of(i * 64, 64), 64)
+            nland[block, :] = (resid[block, :] + (bown[block, :] + bland[block, :].astype(F32))).astype(BF16)
+            return carry
+
+        lax.fori_loop(0, 8, layer_out, 0)
+        send(nland, bo_rows, y_s.at[7], y_r.at[7], dev_y)
+        pltpu.make_async_copy(nland, bo_rows, loc_sem.at[1]).start()
+
+    after = {
+        0: [(Q1, 0), (R3, 1), (R3, 2)],
+        1: [(Q1, 1), (Q2, 0), (R3, 3), (R4, 0), (R4, 1)],
+        2: [(Q1, 2), (Q2, 1), (R3, 4), (R4, 2), (emit_out, 0)],
+        3: [(Q1, 3), (Q2, 2)],
+    }
+    R3(0)
 
     def attention_back_step(h, carry):
         backward_chunk(h)
@@ -662,13 +699,11 @@
 
     def norm_one_back(i, carry):
         block = pl.ds(pl.multiple_of(i * 64, 64), 64)
-        mine = pl.ds(pl.multiple_of(own + i * 64, 64), 64)
-        other = pl.ds(pl.multiple_of(peer + i * 64, 64), 64)
         values = tok[block, :].astype(F32)
         factor = row_factor(values)
         normed = values * factor
-        grad = n2b[other, :]
-        back = n2b[mine, :] + factor * (grad - normed * jnp.mean(grad * normed, axis=-1, keepdims=True))
+        grad = pacc[lax.div(i, 4), pl.ds(pl.multiple_of(lax.rem(i, 4) * 64, 64), 64), :]
+        back = nown[block, :] + factor * (grad - normed * jnp.mean(grad * normed, axis=-1, keepdims=True))
         in1[block, :] = back.astype(BF16)
         return carry
 
@@ -679,24 +714,8 @@
     keep_gt.start()
     Q2(ATT_CHUNKS - 1)
 
-    for part in range(2):
-        got(half_rows(bland, part), y_s.at[4 + part], y_r.at[4 + part])
-
-    def layer_out(i, carry):
-        block = pl.ds(pl.multiple_of(i * 64, 64), 64)
-        mine = pl.ds(pl.multiple_of(own + i * 64, 64), 64)
-        nland[block, :] = (resid[block, :] + (b2[mine, :] + bland[block, :].astype(F32))).astype(BF16)
-        return carry
-
-    lax.fori_loop(0, 8, layer_out, 0)
-    bo_rows = bo_hbm.at[pl.ds(own, 512)]
-    send(nland, bo_rows, y_s.at[7], y_r.at[7], dev_y)
-    keep_bo = pltpu.make_async_copy(nland, bo_rows, loc_sem.at[1])
-    keep_bo.start()
-
-    for j in range(ATT_CHUNKS, ff_chunks):
-        R3(j)
-    for j in range(ATT_CHUNKS - 1, ff_chunks):
+    R3(5)
+    for j in range(3, ff_chunks):
         R4(j)
     Q3(0)
     Q3(1)
@@ -718,7 +737,7 @@
     got(gt_hbm.at[pl.ds(peer, 512)], y_s.at[6], y_r.at[6])
     got(bo_hbm.at[pl.ds(peer, 512)], y_s.at[7], y_r.at[7])
     keep_gt.wait()
-    keep_bo.wait()
+    pltpu.make_async_copy(nland, bo_rows, loc_sem.at[1]).wait()
     for j in range(ff_chunks):
         r_sent(j)
     for h in range(ATT_CHUNKS):
@@ -754,15 +773,15 @@
         vm((width, count), BF16),
         vm((count, width), BF16),
         vm((width, count), BF16),
-        vm((count, width), F32),
-        vm((count, width), F32),
-        vm((3, count, WIDE), BF16),
+        vm((half, width), F32),
+        vm((half, width), F32),
+        vm((2, WIDE, width), F32),
+        vm((3, ff_chunks, count, WIDE), BF16),
         vm((half, width), BF16),
         vm((half, width), BF16),
-        vm((2, 3, NZ, 2, ROWS, WIDE), BF16),
+        vm((2, 4, NZ, 2, ROWS, WIDE), BF16),
         vm((ff_chunks, 3, NZ, ROWS, WIDE), BF16),
         vm((ff_chunks, 3, 3, ROWS, WIDE), BF16),
-        vm((2, 4, NZ, 2, ROWS, WIDE), BF16),
         vm((ATT_CHUNKS, 4, NZ, ROWS, WIDE), BF16),
         vm((ATT_CHUNKS, 3, 4, ROWS, WIDE), BF16),
         vm((ATT_CHUNKS, 4, ROWS, HALF), BF16),
@@ -780,7 +799,6 @@
         dma((8,)),
         dma((8,)),
         dma((ff_chunks + ATT_CHUNKS,)),
-        pltpu.SemaphoreType.REGULAR,
         pltpu.SemaphoreType.REGULAR,
     ]
     anywhere = pl.BlockSpec(memory_space=pl.ANY)
@@ -822,7 +840,7 @@
         and tokens == (16384, 1024)
         and w_query == (1024, 1024)
         and w_gate[1] % (2 * HALF) == 0
-        and w_gate[1] // 2 <= 6 * WIDE
+        and 5 * WIDE < w_gate[1] // 2 <= 6 * WIDE
     )
 
 

time: 286 us -> 263 us (0.920)
  Pallas kernels: 268 us -> 246 us
    pallas_call x1, Pallas kernels: 268 us -> 246 us  [fast_body(): pl.pallas_call(functools.partial(layer_kernel, ff_chunks, ff_width), out_...]
where the time goes in v2:
time: 263 us
  Pallas kernels  246 us (94%)
  local copies, waits for them, and re-layouts  13.8 us (5%)
    pallas_call x1, Pallas kernels, fast_body(): pl.pallas_call(functools.partial(layer_kernel, ff_chunks, ff_width), out_...  246 us

profile of v2, /device:TPU:0, one launch (start us, length us, event | category | flops | bytes accessed | tf_op | source)
XLA Modules:
  0.0 262.6 jit_solution(8387932961909414509)
XLA Ops:
  0.6 0.0 copy-start.3
  0.7 0.9 bitcast_bitcast_fusion.4
  1.6 0.9 bitcast_bitcast_fusion.6
  2.5 0.7 pad_maximum_fusion.1.ash
  3.2 0.9 pad.11
  4.2 0.9 pad.12
  5.2 0.0 copy-done.3
  5.2 0.9 pad_maximum_fusion.ssh
  6.1 246.5 %layer.1 = (bf16[1024,1024]{1,0:T(8,128)(2,1)}, bf16[1024,1024]{1,0:T(8,128)(2,1)}, f32[4,4,64,128]{3,2,1,0:T(8,128)}, f32[6,3,64,256]{3,2,1,0:T(8,128)}) custom-call(bf16[1024,1024]{1,0:T(8,128)(2,1)} %tok_hbm.1, bf16[1024,1024]{1,0:T(8,128)(2,1)} %og_hbm.1, bf16[4,4,64,128]{3,2,1,0:T(8,128)(2,1)} %pad_maximum_fusion.1.ash, ...), custom_call_target="tpu_custom_call" | custom-call | tf_op jit(solution)/shard_map/layer/pallas_call | solution.py:805
  252.6 0.0 copy-start.2
  252.6 1.2 slice_bitcast_fusion.4
  253.8 0.7 copy.58
  254.5 0.7 copy.59
  255.1 0.7 copy.60
  255.8 0.7 copy.61
  256.5 0.0 copy-done.2
  256.5 0.1 slice_bitcast_fusion
  256.6 0.0 copy-start.1
  256.6 0.8 slice.40
  257.4 0.8 slice.41
  258.2 0.8 slice_bitcast_fusion.3
  259.0 0.0 copy-done.1
  259.0 0.0 copy-start
  259.0 1.3 copy.64
  260.3 1.0 copy-done
  261.3 1.3 copy.65
  (6 shorter events, 0.1 us)
Async XLA Ops:
  0.6 4.5 %copy-start.3 = (bf16[64,1408]{1,0:T(8,128)(2,1)S(1)}, bf16[64,1408]{1,0:T(8,128)(2,1)}, u32[]{:S(2)}) copy-start(bf16[64,1408]{1,0:T(8,128)(2,1)} %param.14) | copy-start | bytes 540676
  252.6 3.9 %copy-start.2 = (f32[6,3,64,256]{3,2,1,0:T(8,128)S(1)}, f32[6,3,64,256]{3,2,1,0:T(8,128)}, u32[]{:S(2)}) copy-start(f32[6,3,64,256]{3,2,1,0:T(8,128)} %get-tuple-element.16) | copy-start | bytes 3538948
  256.6 2.4 copy-start.1
  259.0 2.3 copy-start
